TPU v7x, 32 devices: a whole 2x2x4 slice. The times are simulated.
32 devices in a mesh: sp: 4 (over y, x), fsdp: 8 (over z, core).
Axes of the slice: x: 2, y: 2, z: 4, core: 2. Of those that a mesh axis runs over, the one named last changes fastest.
Arguments:
- layer_input: bfloat16 [8, 1024, 2048], P('fsdp', 'sp'), may hold values from -6 to 6
- positions: int32 [8, 1024], P('fsdp'), may hold values from 0 to 1023, as said below
- cotangent: bfloat16 [8, 1024, 2048], P('fsdp', 'sp'), may hold values from -6 to 6
- w_qkv: bfloat16 [2048, 1536], P('fsdp'), may hold values from -0.125 to 0.125
- w_out: bfloat16 [1024, 2048], P('fsdp'), may hold values from -1 to 1
- w_gate: bfloat16 [2048, 4096], P('fsdp'), may hold values from -0.125 to 0.125
- w_up: bfloat16 [2048, 4096], P('fsdp'), may hold values from -0.125 to 0.125
- w_down: bfloat16 [4096, 2048], P('fsdp'), may hold values from -0.09375 to 0.09375
- gain_attn: bfloat16 [2048], P('fsdp'), may hold values from 0.099609375 to 1.8984375
- gain_ffn: bfloat16 [2048], P('fsdp'), may hold values from 0.099609375 to 1.8984375
- gain_query: bfloat16 [64], replicated, may hold values from 1 to 2
- gain_key: bfloat16 [64], replicated, may hold values from 1 to 2
Outputs:
- out: bfloat16 [8, 1024, 2048], P('fsdp', 'sp')
- grad_input: float32 [8, 1024, 2048], P('fsdp', 'sp')
- grad_qkv: float32 [2048, 1536], P(('sp', 'fsdp'))
- grad_out: float32 [1024, 2048], P(('sp', 'fsdp'))
- grad_gate: float32 [2048, 4096], P(('sp', 'fsdp'))
- grad_up: float32 [2048, 4096], P(('sp', 'fsdp'))
- grad_down: float32 [4096, 2048], P(('sp', 'fsdp'))
- grad_gain_attn: float32 [2048], P(('sp', 'fsdp'))
- grad_gain_ffn: float32 [2048], P(('sp', 'fsdp'))
- grad_gain_query: float32 [64], replicated
- grad_gain_key: float32 [64], replicated
Inputs may be any that keep to these rules, and one draw needn't show every extreme that they name: `positions`: in each sequence the first position is 0, and every later position is either 0 (a new document starts) or the previous position plus 1. The first sequence is a single document.
All inputs are finite; a program needn't handle non-finite values.
Results may differ from a plain program's by a relative error of at most 0.015.
The roundings to bfloat16 on the way count: a program that leaves them out, or rounds other values in their place, can miss the bound.
Values may be sent and summed in bfloat16 or wider, within the bound.
A program may use at most 320 MiB of HBM per device.

v0:
```python
import jax
import jax.numpy as jnp
from jax import lax
from jax.sharding import PartitionSpec as P

QUERY_HEAD_COUNT = 16
KEY_VALUE_HEADS = 4
HEAD_DIMENSION = 64


epsilon = 1e-06


def rms_scale(values, weight_gain):
    return (
        values
        * lax.rsqrt(jnp.mean(values * values, axis=-1, keepdims=True) + epsilon)
        * weight_gain
    )


def rope_tables(position_ids, head_size):
    half_dim = head_size // 2
    frequency = 10000.0 ** (-2.0 * jnp.arange(half_dim, dtype=jnp.float32) / head_size)
    angles = position_ids.astype(jnp.float32)[:, None, None] * frequency
    return (jnp.cos(angles), jnp.sin(angles))


def rotate(values, cosine, sine_part):
    half_dim = values.shape[-1] // 2
    front_part = values[..., :half_dim]
    back_part = values[..., half_dim:]
    return jnp.concatenate(
        [front_part * cosine - back_part * sine_part, back_part * cosine + front_part * sine_part],
        axis=-1,
    )


def head_prep(raw_heads, head_gain, cosine, sine_part):
    return rotate(rms_scale(raw_heads, head_gain), cosine, sine_part)


def over_rows(left_side, right_side):
    return lax.dot_general(
        left_side, right_side, (((0,), (0,)), ((), ())), preferred_element_type=jnp.float32
    )


def times_transposed(left_side, right_side):
    return lax.dot_general(
        left_side, right_side, (((1,), (1,)), ((), ())), preferred_element_type=jnp.float32
    )


def masked_scores(query_rows, keys, position_ids):
    sequence_length = query_rows.shape[0]
    scores = jnp.einsum(
        "qkgd,tkd->kgqt", query_rows, keys, preferred_element_type=jnp.float32
    ) * query_rows.shape[-1] ** (-0.5)
    query_index = jnp.arange(sequence_length, dtype=jnp.int32)[:, None]
    key_index = jnp.arange(sequence_length, dtype=jnp.int32)[None, :]
    allowed = (key_index <= query_index) & (query_index - key_index <= position_ids[:, None])
    return (jnp.where(allowed, scores, -1e30), allowed)


def attend(query_rows, keys, values, position_ids):
    masked, allowed = masked_scores(query_rows, keys, position_ids)
    largest = jnp.max(masked, axis=-1, keepdims=True)
    exponent = jnp.exp(masked - largest)
    row_total = jnp.sum(exponent, axis=-1, keepdims=True)
    probabilities = (exponent / row_total).astype(jnp.bfloat16)
    mixture = jnp.einsum(
        "kgqt,tkd->qkgd", probabilities, values, preferred_element_type=jnp.float32
    )
    return (mixture.astype(jnp.bfloat16), (largest + jnp.log(row_total))[..., 0])


def attend_back(query_rows, keys, values, position_ids, grad_mixture, log_total):
    masked, allowed = masked_scores(query_rows, keys, position_ids)
    probabilities = jnp.exp(masked - log_total[..., None])
    probs_low = probabilities.astype(jnp.bfloat16)
    grad_values = jnp.einsum(
        "kgqt,qkgd->tkd", probs_low, grad_mixture, preferred_element_type=jnp.float32
    )
    grad_probs = jnp.einsum(
        "qkgd,tkd->kgqt", grad_mixture, values, preferred_element_type=jnp.float32
    )
    inner_sum = jnp.sum(grad_probs * probabilities, axis=-1, keepdims=True)
    grad_scores = jnp.where(allowed, probabilities * (grad_probs - inner_sum), 0.0).astype(
        jnp.bfloat16
    )
    score_scale = query_rows.shape[-1] ** (-0.5)
    grad_queries = (
        jnp.einsum("kgqt,tkd->qkgd", grad_scores, keys, preferred_element_type=jnp.float32)
        * score_scale
    )
    grad_keys = (
        jnp.einsum("kgqt,qkgd->tkd", grad_scores, query_rows, preferred_element_type=jnp.float32)
        * score_scale
    )
    return (
        grad_queries.astype(jnp.bfloat16),
        grad_keys.astype(jnp.bfloat16),
        grad_values.astype(jnp.bfloat16),
    )


def local(
    layer_input,
    positions,
    cotangent,
    w_qkv,
    w_out,
    w_gate,
    w_up,
    w_down,
    gain_attn,
    gain_ffn,
    gain_query,
    gain_key,
):
    sequence_split_count = lax.axis_size("sp")
    sequence_count, local_length, model_width = layer_input.shape
    full_len = positions.shape[1]
    token_row_count = sequence_count * local_length
    head_copies = max(1, sequence_split_count // KEY_VALUE_HEADS)
    query_dev = QUERY_HEAD_COUNT // sequence_split_count
    slots_per_device = KEY_VALUE_HEADS * head_copies // sequence_split_count
    query_group_width = query_dev // slots_per_device
    qkv_full, out_full, attn_gain = (
        lax.all_gather(w_qkv, "fsdp", axis=0, tiled=True),
        lax.all_gather(w_out, "fsdp", axis=0, tiled=True),
        lax.all_gather(gain_attn, "fsdp", axis=0, tiled=True),
    )
    gate_full, up_full, down_full, ffn_gain = (
        lax.all_gather(w_gate, "fsdp", axis=0, tiled=True),
        lax.all_gather(w_up, "fsdp", axis=0, tiled=True),
        lax.all_gather(w_down, "fsdp", axis=0, tiled=True),
        lax.all_gather(gain_ffn, "fsdp", axis=0, tiled=True),
    )
    inputs = layer_input.reshape(token_row_count, model_width).astype(jnp.float32)
    normed_val, attn_pull = jax.vjp(rms_scale, inputs, attn_gain.astype(jnp.float32))
    normed = normed_val.astype(jnp.bfloat16)
    projected_rows = jnp.dot(normed, qkv_full, preferred_element_type=jnp.float32)
    query_raw = projected_rows[:, : QUERY_HEAD_COUNT * HEAD_DIMENSION].reshape(
        token_row_count, QUERY_HEAD_COUNT, HEAD_DIMENSION
    )
    key_unrotated = projected_rows[
        :, QUERY_HEAD_COUNT * HEAD_DIMENSION : (QUERY_HEAD_COUNT + KEY_VALUE_HEADS) * HEAD_DIMENSION
    ].reshape(token_row_count, KEY_VALUE_HEADS, HEAD_DIMENSION)
    value_unprojected = projected_rows[
        :, (QUERY_HEAD_COUNT + KEY_VALUE_HEADS) * HEAD_DIMENSION :
    ].reshape(token_row_count, KEY_VALUE_HEADS, HEAD_DIMENSION)
    offset = lax.axis_index("sp") * local_length
    local_pos = lax.dynamic_slice_in_dim(positions, offset, local_length, 1).reshape(
        token_row_count
    )
    cosine, sine_part = rope_tables(local_pos, HEAD_DIMENSION)

    def query_fn(raw_heads, head_gain):
        return head_prep(raw_heads, head_gain, cosine, sine_part)

    query_rot, query_pull = jax.vjp(query_fn, query_raw, gain_query.astype(jnp.float32))
    key_rot, key_pull = jax.vjp(query_fn, key_unrotated, gain_key.astype(jnp.float32))
    queries_low = query_rot.astype(jnp.bfloat16).reshape(
        sequence_count, local_length, QUERY_HEAD_COUNT * HEAD_DIMENSION
    )
    keys_low = jnp.repeat(key_rot.astype(jnp.bfloat16), head_copies, axis=1).reshape(
        sequence_count, local_length, KEY_VALUE_HEADS * head_copies * HEAD_DIMENSION
    )
    values_low = jnp.repeat(value_unprojected.astype(jnp.bfloat16), head_copies, axis=1).reshape(
        sequence_count, local_length, KEY_VALUE_HEADS * head_copies * HEAD_DIMENSION
    )
    heads_query, heads_key, heads_value = (
        lax.all_to_all(queries_low, "sp", split_axis=2, concat_axis=1, tiled=True),
        lax.all_to_all(keys_low, "sp", split_axis=2, concat_axis=1, tiled=True),
        lax.all_to_all(values_low, "sp", split_axis=2, concat_axis=1, tiled=True),
    )
    query_heads = heads_query.reshape(
        sequence_count, full_len, slots_per_device, query_group_width, HEAD_DIMENSION
    )
    key_heads = heads_key.reshape(sequence_count, full_len, slots_per_device, HEAD_DIMENSION)
    value_heads = heads_value.reshape(sequence_count, full_len, slots_per_device, HEAD_DIMENSION)
    mixture, log_total = lax.map(
        lambda packed: attend(*packed), (query_heads, key_heads, value_heads, positions)
    )
    mixture_heads = mixture.reshape(sequence_count, full_len, query_dev * HEAD_DIMENSION)
    attn_heads = lax.all_to_all(
        mixture_heads, "sp", split_axis=1, concat_axis=2, tiled=True
    ).reshape(token_row_count, QUERY_HEAD_COUNT * HEAD_DIMENSION)
    middle = inputs + jnp.dot(attn_heads, out_full, preferred_element_type=jnp.float32)
    ffn_val, ffn_pull = jax.vjp(rms_scale, middle, ffn_gain.astype(jnp.float32))
    ffn_in = ffn_val.astype(jnp.bfloat16)
    gate_value = jnp.dot(ffn_in, gate_full, preferred_element_type=jnp.float32)
    up_value = jnp.dot(ffn_in, up_full, preferred_element_type=jnp.float32)

    def gated_fn(gate_in, up_in):
        return jax.nn.silu(gate_in) * up_in

    hidden_val, hidden_pull = jax.vjp(gated_fn, gate_value, up_value)
    hidden = hidden_val.astype(jnp.bfloat16)
    result = middle + jnp.dot(hidden, down_full, preferred_element_type=jnp.float32)
    output = result.astype(jnp.bfloat16).reshape(sequence_count, local_length, model_width)
    grad_low = cotangent.reshape(token_row_count, model_width)
    grad_down = over_rows(hidden, grad_low)
    grad_hidden = times_transposed(grad_low, down_full)
    grad_gate_val, grad_up_val = hidden_pull(grad_hidden)
    grad_gate_low = grad_gate_val.astype(jnp.bfloat16)
    grad_up_low = grad_up_val.astype(jnp.bfloat16)
    grad_gate = over_rows(ffn_in, grad_gate_low)
    grad_up = over_rows(ffn_in, grad_up_low)
    grad_ffn_in = times_transposed(grad_gate_low, gate_full) + times_transposed(
        grad_up_low, up_full
    )
    grad_middle_part, grad_ffn_gain = ffn_pull(grad_ffn_in)
    grad_middle = grad_low.astype(jnp.float32) + grad_middle_part
    grad_attn_low = grad_middle.astype(jnp.bfloat16)
    grad_out = over_rows(attn_heads, grad_attn_low)
    grad_mixture_tok = (
        times_transposed(grad_attn_low, out_full)
        .astype(jnp.bfloat16)
        .reshape(sequence_count, local_length, QUERY_HEAD_COUNT * HEAD_DIMENSION)
    )
    grad_mixture = lax.all_to_all(
        grad_mixture_tok, "sp", split_axis=2, concat_axis=1, tiled=True
    ).reshape(sequence_count, full_len, slots_per_device, query_group_width, HEAD_DIMENSION)
    back_query, back_key, back_value = lax.map(
        lambda packed: attend_back(*packed),
        (query_heads, key_heads, value_heads, positions, grad_mixture, log_total),
    )
    tok_query, token_key, token_value = (
        lax.all_to_all(
            back_query.reshape(sequence_count, full_len, query_dev * HEAD_DIMENSION),
            "sp",
            split_axis=1,
            concat_axis=2,
            tiled=True,
        ),
        lax.all_to_all(
            back_key.reshape(sequence_count, full_len, slots_per_device * HEAD_DIMENSION),
            "sp",
            split_axis=1,
            concat_axis=2,
            tiled=True,
        ),
        lax.all_to_all(
            back_value.reshape(sequence_count, full_len, slots_per_device * HEAD_DIMENSION),
            "sp",
            split_axis=1,
            concat_axis=2,
            tiled=True,
        ),
    )
    grad_key_rotated = jnp.sum(
        token_key.reshape(token_row_count, KEY_VALUE_HEADS, head_copies, HEAD_DIMENSION).astype(
            jnp.float32
        ),
        axis=2,
    )
    grad_value_rows = jnp.sum(
        token_value.reshape(token_row_count, KEY_VALUE_HEADS, head_copies, HEAD_DIMENSION).astype(
            jnp.float32
        ),
        axis=2,
    )
    grad_query_raw, grad_gain_query = query_pull(
        tok_query.reshape(token_row_count, QUERY_HEAD_COUNT, HEAD_DIMENSION).astype(jnp.float32)
    )
    grad_key_unrotated, grad_gain_key = key_pull(grad_key_rotated)
    grad_projected = jnp.concatenate(
        [
            grad_query_raw.reshape(token_row_count, QUERY_HEAD_COUNT * HEAD_DIMENSION),
            grad_key_unrotated.reshape(token_row_count, KEY_VALUE_HEADS * HEAD_DIMENSION),
            grad_value_rows.reshape(token_row_count, KEY_VALUE_HEADS * HEAD_DIMENSION),
        ],
        axis=1,
    ).astype(jnp.bfloat16)
    grad_qkv = over_rows(normed, grad_projected)
    grad_normed = times_transposed(grad_projected, qkv_full)
    grad_input_part, grad_attn_gain = attn_pull(grad_normed)
    grad_input = (grad_middle + grad_input_part).reshape(sequence_count, local_length, model_width)
    share_qkv, share_out, share_gate, share_up, share_down, share_attn_gain, share_ffn_gain = (
        lax.psum_scatter(grad_qkv, ("sp", "fsdp"), scatter_dimension=0, tiled=True),
        lax.psum_scatter(grad_out, ("sp", "fsdp"), scatter_dimension=0, tiled=True),
        lax.psum_scatter(grad_gate, ("sp", "fsdp"), scatter_dimension=0, tiled=True),
        lax.psum_scatter(grad_up, ("sp", "fsdp"), scatter_dimension=0, tiled=True),
        lax.psum_scatter(grad_down, ("sp", "fsdp"), scatter_dimension=0, tiled=True),
        lax.psum_scatter(grad_attn_gain, ("sp", "fsdp"), scatter_dimension=0, tiled=True),
        lax.psum_scatter(grad_ffn_gain, ("sp", "fsdp"), scatter_dimension=0, tiled=True),
    )
    sum_gain_query, sum_gain_key = lax.psum((grad_gain_query, grad_gain_key), ("sp", "fsdp"))
    return (
        output,
        grad_input,
        share_qkv,
        share_out,
        share_gate,
        share_up,
        share_down,
        share_attn_gain,
        share_ffn_gain,
        sum_gain_query,
        sum_gain_key,
    )


def solution(mesh):
    placed = (
        P("fsdp", "sp", None),
        P("fsdp", None),
        P("fsdp", "sp", None),
        P("fsdp", None),
        P("fsdp", None),
        P("fsdp", None),
        P("fsdp", None),
        P("fsdp", None),
        P("fsdp"),
        P("fsdp"),
        P(),
        P(),
    )
    return jax.shard_map(
        local,
        mesh=mesh,
        in_specs=placed,
        out_specs=(
            P("fsdp", "sp", None),
            P("fsdp", "sp", None),
            P(("sp", "fsdp"), None),
            P(("sp", "fsdp"), None),
            P(("sp", "fsdp"), None),
            P(("sp", "fsdp"), None),
            P(("sp", "fsdp"), None),
            P(("sp", "fsdp")),
            P(("sp", "fsdp")),
            P(),
            P(),
        ),
        check_vma=False,
    )
```

profile of v0, /device:TPU:0, one launch (start us, length us, event | category | flops | bytes accessed | tf_op | source)
XLA Modules:
  0.0 2028.1 jit_solution(921883647904297051)
XLA Ops:
  10.7 13.4 all-gather
  25.3 51.9 %all-gather.8.cloned.1.call-done = bf16[2048,1536]{1,0:T(8,128)(2,1)} async-done(((bf16[256,1536]{1,0:T(8,128)(2,1)}), bf16[2048,1536]{1,0:T(8,128)(2,1)}) %all-gather.8.cloned.1.call-update) | async-done | bytes 6291472 | tf_op jit(solution)/shard_map/all_gather | solution.py:131
  135.0 8.7 fusion.30
  152.9 10.3 all-gather.1
  168.9 107.2 %all-gather.14.cloned.1.call-done = bf16[2048,4096]{1,0:T(8,128)(2,1)} async-done(((bf16[256,4096]{1,0:T(8,128)(2,1)}), bf16[2048,4096]{1,0:T(8,128)(2,1)}) %all-gather.14.cloned.1.call-update) | async-done | bytes 16777232 | tf_op jit(solution)/shard_map/all_gather | solution.py:137
  276.2 10.1 fusion.69
  286.3 140.7 %all-gather.12.cloned.1.call-done = bf16[2048,4096]{1,0:T(8,128)(2,1)} async-done(((bf16[256,4096]{1,0:T(8,128)(2,1)}), bf16[2048,4096]{1,0:T(8,128)(2,1)}) %all-gather.12.cloned.1.call-update) | async-done | bytes 16777232 | tf_op jit(solution)/shard_map/all_gather | solution.py:136
  427.0 10.2 fusion.68
  437.2 140.6 %all-gather.16.cloned.1.call-done = bf16[4096,2048]{1,0:T(8,128)(2,1)} async-done(((bf16[512,2048]{1,0:T(8,128)(2,1)}), bf16[4096,2048]{1,0:T(8,128)(2,1)}) %all-gather.16.cloned.1.call-update) | async-done | bytes 16777232 | tf_op jit(solution)/shard_map/all_gather | solution.py:138
  577.8 13.7 multiply_convert_fusion
  591.5 12.2 fusion.70
  603.7 13.8 multiply_reduce_fusion
  643.0 11.2 all-to-all-done.4
  657.2 8.6 fusion.43
  680.7 10.9 fusion.9
  755.5 14.9 fusion.47
  771.7 15.0 fusion.72
  786.7 17.0 fusion.71
  803.8 13.7 fusion.21
  823.9 40.4 %all-reduce.6 = (f32[2048]{0:T(1024)S(1)}, f32[2048]{0:T(1024)S(1)}, f32[64]{0:T(128)}, f32[64]{0:T(128)}) all-reduce(f32[2048]{0:T(1024)S(1)} %get-tuple-element.54, f32[2048]{0:T(1024)S(1)} %copy-done.38, f32[64]{0:T(128)S(1)} %get-tuple-element.56, f32[64]{0:T(128)S(1)} %get-tuple-element.68), channel_id=7, replica_groups=mesh['sp'=4,'fsdp'=8] {'sp','fsdp'}, use_global_device_ids=true, to_apply=%region_17.18.clone | all-reduce | flops 4224 | bytes 33792
  869.0 67.6 %reduce-scatter.6.cloned.1.call-done = f32[64,1536]{1,0:T(8,128)} async-done(((f32[2048,1536]{1,0:T(8,128)}), f32[64,1536]{1,0:T(8,128)}) %reduce-scatter.6.cloned.1.call-update) | async-done | bytes 393232 | tf_op jit(solution)/shard_map/reduce_scatter | solution.py:283
  936.6 363.2 %reduce-scatter.14.cloned.1.call-done = f32[128,2048]{1,0:T(8,128)} async-done(((f32[4096,2048]{1,0:T(8,128)}), f32[128,2048]{1,0:T(8,128)}) %reduce-scatter.14.cloned.1.call-update) | async-done | bytes 1048592 | tf_op jit(solution)/shard_map/reduce_scatter | solution.py:287
  1299.7 360.6 %reduce-scatter.12.cloned.1.call-done = f32[64,4096]{1,0:T(8,128)} async-done(((f32[2048,4096]{1,0:T(8,128)}), f32[64,4096]{1,0:T(8,128)}) %reduce-scatter.12.cloned.1.call-update) | async-done | bytes 1048592 | tf_op jit(solution)/shard_map/reduce_scatter | solution.py:286
  1660.4 360.5 %reduce-scatter.10.cloned.1.call-done = f32[64,4096]{1,0:T(8,128)} async-done(((f32[2048,4096]{1,0:T(8,128)}), f32[64,4096]{1,0:T(8,128)}) %reduce-scatter.10.cloned.1.call-update) | async-done | bytes 1048592 | tf_op jit(solution)/shard_map/reduce_scatter | solution.py:285
  (244 shorter events, 196.0 us)
Async XLA Ops:
  7.2 70.0 %all-gather.8.cloned.1.call-start = ((), (), s32[]{:S(2)}) async-start(), calls=%async_computation.13 | async-start | bytes 7077888 | tf_op jit(solution)/shard_map/all_gather | solution.py:131
  8.0 156.9 %all-gather.10.cloned.1.call-start = ((), (), s32[]{:S(2)}) async-start(), calls=%async_computation.14 | async-start | bytes 4718592 | tf_op jit(solution)/shard_map/all_gather | solution.py:132
  8.7 267.4 %all-gather.14.cloned.1.call-start = ((), (), s32[]{:S(2)}) async-start(), calls=%async_computation.16 | async-start | bytes 18874368 | tf_op jit(solution)/shard_map/all_gather | solution.py:137
  9.4 417.5 %all-gather.12.cloned.1.call-start = ((), (), s32[]{:S(2)}) async-start(), calls=%async_computation.15 | async-start | bytes 18874368 | tf_op jit(solution)/shard_map/all_gather | solution.py:136
  10.0 567.8 %all-gather.16.cloned.1.call-start = ((), (), s32[]{:S(2)}) async-start(), calls=%async_computation.17 | async-start | bytes 18874368 | tf_op jit(solution)/shard_map/all_gather | solution.py:138
  10.6 80.0 %copy-start.40 = (f32[64]{0:T(128)}, f32[64]{0:T(128)S(1)}, u32[]{:S(2)}) copy-start(f32[64]{0:T(128)S(1)} %convert_element_type.184) | copy-start | bytes 772
  10.7 79.4 %copy-start.42 = (f32[64]{0:T(128)}, f32[64]{0:T(128)S(1)}, u32[]{:S(2)}) copy-start(f32[64]{0:T(128)S(1)} %convert_element_type.180) | copy-start | bytes 772
  25.3 65.7 %copy-start.18 = (f32[256,32]{0,1:T(8,128)}, f32[256,32]{0,1:T(8,128)S(1)}, u32[]{:S(2)}) copy-start(f32[256,32]{0,1:T(8,128)S(1)} %get-tuple-element.85) | copy-start | bytes 98308
  25.3 65.7 %copy-start.20 = (f32[256,32]{0,1:T(8,128)}, f32[256,32]{0,1:T(8,128)S(1)}, u32[]{:S(2)}) copy-start(f32[256,32]{0,1:T(8,128)S(1)} %get-tuple-element.86) | copy-start | bytes 98308
  84.8 9.0 all-to-all-start
  93.8 9.4 all-to-all-start.1
  103.2 12.8 all-to-all-start.2
  149.3 13.9 all-to-all-start.3
  152.8 716.1 %reduce-scatter.8.cloned.1.call-start = ((), (), s32[]{:S(2)}) async-start(), calls=%async_computation.19 | async-start | bytes 8650752 | tf_op jit(solution)/shard_map/reduce_scatter | solution.py:284
  168.7 435.0 %copy-start.2 = (f32[256,2048]{1,0:T(8,128)}, f32[256,2048]{1,0:T(8,128)S(1)}, u32[]{:S(2)}) copy-start(f32[256,2048]{1,0:T(8,128)S(1)} %get-tuple-element.90) | copy-start | bytes 6291460
  168.9 258.1 %copy-start.6 = (bf16[256,2048]{1,0:T(8,128)(2,1)}, bf16[256,2048]{1,0:T(8,128)(2,1)S(1)}, u32[]{:S(2)}) copy-start(bf16[256,2048]{1,0:T(8,128)(2,1)S(1)} %multiply_convert_fusion.2) | copy-start | bytes 3145732
  638.8 15.3 all-to-all-start.4
  669.4 31.9 %all-to-all-start.7 = ((bf16[4,2,8192]{2,1,0:T(2,128)(2,1)}), bf16[4,2,8192]{2,1,0:T(2,128)(2,1)S(1)}, u32[]{:S(2)}, u32[]{:S(2)}) async-start(bf16[4,2,8192]{2,1,0:T(2,128)(2,1)} %reshape.422), calls=%async_computation.7 | async-start | bytes 262144 | tf_op jit(solution)/shard_map/all_to_all | solution.py:246
  701.3 20.6 %all-to-all-start.6 = ((bf16[4,2,8192]{2,1,0:T(2,128)(2,1)}), bf16[4,2,8192]{2,1,0:T(2,128)(2,1)}, u32[]{:S(2)}, u32[]{:S(2)}) async-start(bf16[4,2,8192]{2,1,0:T(2,128)(2,1)} %reshape.424), calls=%async_computation.6 | async-start | bytes 262144 | tf_op jit(solution)/shard_map/all_to_all | solution.py:239
  721.9 14.5 all-to-all-start.5
  726.3 210.2 %reduce-scatter.6.cloned.1.call-start = ((), (), s32[]{:S(2)}) async-start(), calls=%async_computation.18 | async-start | bytes 12976128 | tf_op jit(solution)/shard_map/reduce_scatter | solution.py:283
  754.3 545.4 %reduce-scatter.14.cloned.1.call-start = ((), (), s32[]{:S(2)}) async-start(), calls=%async_computation.22 | async-start | bytes 34603008 | tf_op jit(solution)/shard_map/reduce_scatter | solution.py:287
  770.5 889.9 %reduce-scatter.12.cloned.1.call-start = ((), (), s32[]{:S(2)}) async-start(), calls=%async_computation.21 | async-start | bytes 34603008 | tf_op jit(solution)/shard_map/reduce_scatter | solution.py:286
  786.7 1234.2 %reduce-scatter.10.cloned.1.call-start = ((), (), s32[]{:S(2)}) async-start(), calls=%async_computation.20 | async-start | bytes 34603008 | tf_op jit(solution)/shard_map/reduce_scatter | solution.py:285
  (42 other events, 510.7 us)
Sparse Core Ops, SparseCore 0:
  9.7 67.4 all-gather.7
  78.8 45.7 all-gather.9
  126.2 149.8 all-gather.13
  277.6 149.3 all-gather.11
  428.4 149.3 all-gather.15
  625.3 150.3 reduce-scatter.7
  782.3 154.2 reduce-scatter.5
  939.5 360.1 reduce-scatter.13
  1302.7 357.6 reduce-scatter.11
  1663.2 357.6 reduce-scatter.9
where the time goes:
time: 2040 us; the launch traced here: 2030 us
  waiting for transfers between devices  1620 us (79%)
  matrix products  195 us (10%)
  blocking collectives  64.1 us (3%)
  other arithmetic  55.9 us (3%)
  local copies, waits for them, and re-layouts  44 us (2%)
  starting transfers between devices  32.5 us (2%)
    reduce_scatter x1, waiting for transfers between devices, local(): lax.psum_scatter(grad_down, ('sp', 'fsdp'), scatter_dimension=0, tiled=True)  363 us
    reduce_scatter x1, waiting for transfers between devices, local(): lax.psum_scatter(grad_up, ('sp', 'fsdp'), scatter_dimension=0, tiled=True)  361 us
    reduce_scatter x1, waiting for transfers between devices, local(): lax.psum_scatter(grad_gate, ('sp', 'fsdp'), scatter_dimension=0, tiled=True)  360 us
    all_gather x1, waiting for transfers between devices, local(): lax.all_gather(w_gate, 'fsdp', axis=0, tiled=True)  141 us
    all_gather x1, waiting for transfers between devices, local(): lax.all_gather(w_down, 'fsdp', axis=0, tiled=True)  141 us
    all_gather x1, waiting for transfers between devices, local(): lax.all_gather(w_up, 'fsdp', axis=0, tiled=True)  107 us
    reduce_scatter x1, waiting for transfers between devices, local(): lax.psum_scatter(grad_qkv, ('sp', 'fsdp'), scatter_dimension=0, tiled=True)  67.6 us
    dot_general x5, matrix products, over_rows(): lax.dot_general(left_side, right_side, (((0,), (0,)), ((), ())), preferre...  57.8 us
  transfers between devices with their start and end apart: 18, of which 12 were waited for; matrix products, arithmetic and copies ran while one was open for 12% of the time, Pallas kernels for 0%

commit v1 on v0

v1 whole, which is shorter than its diff:
```python
import jax
import jax.numpy as jnp
from jax import lax
from jax.sharding import PartitionSpec as P

QUERY_HEADS = 16
KV_HEADS = 4
HD = 64
EPS = 1e-06
f32 = jnp.float32
bf16 = jnp.bfloat16


def rms_scale(values, gain):
    return values * lax.rsqrt(jnp.mean(values * values, axis=-1, keepdims=True) + EPS) * gain


def rope_tables(position_ids):
    half = HD // 2
    frequency = 10000.0 ** (-2.0 * jnp.arange(half, dtype=f32) / HD)
    angles = position_ids.astype(f32)[:, None, None] * frequency
    return jnp.cos(angles), jnp.sin(angles)


def rotate(values, cosine, sine):
    half = HD // 2
    front, back = values[..., :half], values[..., half:]
    return jnp.concatenate([front * cosine - back * sine, back * cosine + front * sine], axis=-1)


def over_rows(a, b):
    return lax.dot_general(a, b, (((0,), (0,)), ((), ())), preferred_element_type=f32)


def times_transposed(a, b):
    return lax.dot_general(a, b, (((1,), (1,)), ((), ())), preferred_element_type=f32)


def masked_scores(q, k, position_ids):
    length = q.shape[0]
    scores = jnp.einsum("qgd,td->gqt", q, k, preferred_element_type=f32) * HD ** (-0.5)
    qi = jnp.arange(length, dtype=jnp.int32)[:, None]
    ki = jnp.arange(length, dtype=jnp.int32)[None, :]
    allowed = (ki <= qi) & (qi - ki <= position_ids[:, None])
    return jnp.where(allowed, scores, -1e30), allowed


def attend(q, k, v, position_ids):
    masked, _ = masked_scores(q, k, position_ids)
    largest = jnp.max(masked, axis=-1, keepdims=True)
    exponent = jnp.exp(masked - largest)
    total = jnp.sum(exponent, axis=-1, keepdims=True)
    probs = (exponent / total).astype(bf16)
    mixture = jnp.einsum("gqt,td->qgd", probs, v, preferred_element_type=f32)
    return mixture.astype(bf16), (largest + jnp.log(total))[..., 0]


def attend_back(q, k, v, position_ids, grad_mixture, log_total):
    masked, allowed = masked_scores(q, k, position_ids)
    probs = jnp.exp(masked - log_total[..., None])
    grad_v = jnp.einsum("gqt,qgd->td", probs.astype(bf16), grad_mixture, preferred_element_type=f32)
    grad_p = jnp.einsum("qgd,td->gqt", grad_mixture, v, preferred_element_type=f32)
    inner = jnp.sum(grad_p * probs, axis=-1, keepdims=True)
    grad_s = jnp.where(allowed, probs * (grad_p - inner), 0.0).astype(bf16)
    scale = HD ** (-0.5)
    grad_q = jnp.einsum("gqt,td->qgd", grad_s, k, preferred_element_type=f32) * scale
    grad_k = jnp.einsum("gqt,qgd->td", grad_s, q, preferred_element_type=f32) * scale
    return grad_q.astype(bf16), grad_k.astype(bf16), grad_v.astype(bf16)


def swap(value, mask, count):
    return lax.ppermute(value, "sp", [(i, i ^ mask) for i in range(count)])


def gather_chunks(chunk, s, count):
    if count != 4:
        return lax.all_gather(chunk, "sp", axis=0)
    half = chunk.shape[0] // 2
    over_x = swap(chunk, 1, count)
    over_y = swap(chunk, 2, count)
    first = swap(over_x[:half], 2, count)
    second = swap(over_y[half:], 1, count)
    stack = jnp.zeros((count,) + chunk.shape, chunk.dtype)
    for mask, part in ((0, chunk), (1, over_x), (2, over_y)):
        stack = lax.dynamic_update_slice_in_dim(stack, part[None], s ^ mask, 0)
    across = jnp.concatenate([first, second], axis=0)
    return lax.dynamic_update_slice_in_dim(stack, across[None], s ^ 3, 0)


def scatter_sum(partial, s, count):
    rows = partial.shape[0] // count
    if count != 4:
        return lax.psum_scatter(partial.astype(bf16), "sp", scatter_dimension=0, tiled=True).astype(f32)
    half = rows // 2

    def part(mask):
        return lax.dynamic_slice_in_dim(partial, (s ^ mask) * rows, rows, 0)

    across = part(3).astype(bf16)
    from_y = swap(across[:half], 2, count)
    from_x = swap(across[half:], 1, count)
    to_x, to_y = part(1), part(2)
    to_x = jnp.concatenate([to_x[:half] + from_y.astype(f32), to_x[half:]], axis=0).astype(bf16)
    to_y = jnp.concatenate([to_y[:half], to_y[half:] + from_x.astype(f32)], axis=0).astype(bf16)
    return part(0) + swap(to_x, 1, count).astype(f32) + swap(to_y, 2, count).astype(f32)


def local(x_own, positions, ct_own, w_qkv, w_out, w_gate, w_up, w_down, gain_attn, gain_ffn, gain_query, gain_key):
    S, F = lax.axis_size("sp"), lax.axis_size("fsdp")
    s = lax.axis_index("sp")
    _, T, D = x_own.shape
    L = positions.shape[1]
    pos = positions[0]
    copies = max(1, S // KV_HEADS)
    QW = QUERY_HEADS * HD
    KW = KV_HEADS * HD
    heads = QUERY_HEADS // S
    qw = heads * HD
    FF = w_gate.shape[1]
    FFs = FF // S
    rows_d = D // (S * F)
    x_own = x_own[0]
    ct_own = ct_own[0]

    def cut(w, start, size, axis):
        return lax.dynamic_slice_in_dim(w, start, size, axis)

    def regroup(w):
        size = w.shape[0] // S
        perm = [(i * F + j, j * S + i) for i in range(S) for j in range(F)]
        return lax.ppermute(cut(w, s * size, size, 0), ("sp", "fsdp"), perm)

    def gather_z(w):
        return lax.all_gather(w, "fsdp", axis=0, tiled=True)

    gains = jnp.pad(jnp.stack([gain_attn, gain_ffn], axis=1), ((0, 0), (0, 126)))
    kv = s // copies
    attn_part = jnp.concatenate(
        [
            cut(w_qkv, s * qw, qw, 1),
            cut(w_qkv, QW + kv * HD, HD, 1),
            cut(w_qkv, QW + KW + kv * HD, HD, 1),
            gains,
        ],
        axis=1,
    )
    attn_full = gather_z(attn_part)
    hw = qw + 2 * HD
    wqkv_s = attn_full[:, :hw]
    g_attn = attn_full[:, hw].astype(f32)
    g_ffn = attn_full[:, hw + 1].astype(f32)
    wout_s = gather_z(regroup(w_out))
    gu_part = jnp.concatenate([cut(w_gate, s * FFs, FFs, 1), cut(w_up, s * FFs, FFs, 1)], axis=1)
    w_gu = gather_z(gu_part)
    w_dn = gather_z(regroup(w_down))

    x_bf = gather_chunks(x_own, s, S).reshape(L, D)
    x_all = x_bf.astype(f32)
    normed = rms_scale(x_all, g_attn).astype(bf16)
    projected = jnp.dot(normed, wqkv_s, preferred_element_type=f32)
    cosine, sine = rope_tables(pos)

    def prep(raw, gain):
        return rotate(rms_scale(raw, gain), cosine, sine)

    q_rot, q_pull = jax.vjp(prep, projected[:, :qw].reshape(L, heads, HD), gain_query.astype(f32))
    k_rot, k_pull = jax.vjp(prep, projected[:, qw : qw + HD].reshape(L, 1, HD), gain_key.astype(f32))
    q = q_rot.astype(bf16)
    k = k_rot.astype(bf16)[:, 0]
    v = projected[:, qw + HD :].astype(bf16)
    mixture, log_total = attend(q, k, v, pos)
    mix_s = mixture.reshape(L, qw)
    mix_all = jnp.swapaxes(gather_chunks(mix_s, s, S), 0, 1).reshape(L, QW)
    wout_full = gather_chunks(wout_s, s, S).reshape(QW, D)
    middle = x_all + jnp.dot(mix_all, wout_full, preferred_element_type=f32)
    ffn_in = rms_scale(middle, g_ffn).astype(bf16)
    gu = jnp.dot(ffn_in, w_gu, preferred_element_type=f32)

    def gated(g, u):
        return jax.nn.silu(g) * u

    hidden_val, hidden_pull = jax.vjp(gated, gu[:, :FFs], gu[:, FFs:])
    hidden = hidden_val.astype(bf16)
    ct_all = gather_chunks(ct_own, s, S).reshape(L, D)
    grad_down = over_rows(hidden, ct_all).astype(bf16)
    grad_down = lax.psum_scatter(grad_down, "fsdp", scatter_dimension=0, tiled=True).astype(f32)

    grad_hidden = times_transposed(ct_all, w_dn)
    d_gate, d_up = hidden_pull(grad_hidden)
    d_gu = jnp.concatenate([d_gate.astype(bf16), d_up.astype(bf16)], axis=1)

    def share_rows(grad):
        width = grad.shape[1]
        grad = grad.astype(bf16).reshape(S, F, rows_d, width)
        grad = jnp.swapaxes(grad, 0, 1).reshape(D, width)
        mine = lax.psum_scatter(grad, "fsdp", scatter_dimension=0, tiled=True)
        mine = mine.reshape(S, rows_d, width)
        return lax.all_to_all(mine, "sp", split_axis=0, concat_axis=0)

    grad_gu = share_rows(over_rows(ffn_in, d_gu))
    grad_gate = jnp.swapaxes(grad_gu[:, :, :FFs], 0, 1).reshape(rows_d, FF).astype(f32)
    grad_up = jnp.swapaxes(grad_gu[:, :, FFs:], 0, 1).reshape(rows_d, FF).astype(f32)

    grad_ffn_in = scatter_sum(times_transposed(d_gu, w_gu), s, S)
    out_sum = scatter_sum(jnp.dot(hidden, w_dn, preferred_element_type=f32), s, S)
    middle_own = cut(middle, s * T, T, 0)
    out = (middle_own + out_sum).astype(bf16)
    _, ffn_pull = jax.vjp(rms_scale, middle_own, g_ffn)
    grad_middle, grad_g_ffn = ffn_pull(grad_ffn_in)
    grad_middle = ct_own.astype(f32) + grad_middle
    d_attn = grad_middle.astype(bf16)

    d_mix_tok = times_transposed(d_attn, wout_full).astype(bf16).reshape(T, S, qw)
    d_mix = lax.all_to_all(jnp.swapaxes(d_mix_tok, 0, 1), "sp", split_axis=0, concat_axis=0)
    d_mix = d_mix.reshape(L, heads, HD)
    d_attn_all = gather_chunks(d_attn, s, S).reshape(L, D)
    grad_out = over_rows(mix_s, d_attn_all).astype(bf16)
    grad_out = lax.psum_scatter(grad_out, "fsdp", scatter_dimension=0, tiled=True).astype(f32)

    dq, dk, dv = attend_back(q, k, v, pos, d_mix, log_total)
    dk, dv = dk.astype(f32), dv.astype(f32)
    if copies > 1:
        groups = [[i * copies + j for j in range(copies)] for i in range(KV_HEADS)]
        dk, dv = lax.psum((dk, dv), "sp", axis_index_groups=groups)
        first = (s % copies == 0).astype(f32)
        dk, dv = dk * first, dv * first
    d_q_raw, grad_g_query = q_pull(dq.astype(f32))
    d_k_raw, grad_g_key = k_pull(dk[:, None])
    d_proj = jnp.concatenate([d_q_raw.reshape(L, qw), d_k_raw[:, 0], dv], axis=1).astype(bf16)

    grad_qkv = share_rows(over_rows(normed, d_proj))
    grad_q = jnp.swapaxes(grad_qkv[:, :, :qw], 0, 1).reshape(rows_d, QW)
    grad_k = jnp.swapaxes(grad_qkv[::copies, :, qw : qw + HD], 0, 1).reshape(rows_d, KW)
    grad_v = jnp.swapaxes(grad_qkv[::copies, :, qw + HD :], 0, 1).reshape(rows_d, KW)
    grad_qkv = jnp.concatenate([grad_q, grad_k, grad_v], axis=1).astype(f32)

    d_proj_own = lax.all_to_all(d_proj.reshape(S, T, hw), "sp", split_axis=0, concat_axis=0)
    wqkv_all = gather_chunks(wqkv_s, s, S)
    grad_normed = jnp.einsum("stc,sdc->td", d_proj_own, wqkv_all, preferred_element_type=f32)
    _, attn_pull = jax.vjp(rms_scale, x_own.astype(f32), g_attn)
    grad_x, grad_g_attn = attn_pull(grad_normed)
    grad_input = grad_middle + grad_x

    tiny = jnp.concatenate([grad_g_attn, grad_g_ffn, grad_g_query, grad_g_key])
    tiny = lax.psum(tiny, ("sp", "fsdp"))
    mine = (s * F + lax.axis_index("fsdp")) * rows_d
    return (
        out[None],
        grad_input[None],
        grad_qkv,
        grad_out,
        grad_gate,
        grad_up,
        grad_down,
        lax.dynamic_slice_in_dim(tiny[:D], mine, rows_d, 0),
        lax.dynamic_slice_in_dim(tiny[D : 2 * D], mine, rows_d, 0),
        tiny[2 * D : 2 * D + HD],
        tiny[2 * D + HD :],
    )


def solution(mesh):
    row = P("fsdp", "sp", None)
    shard = P("fsdp", None)
    grad = P(("sp", "fsdp"), None)
    return jax.shard_map(
        local,
        mesh=mesh,
        in_specs=(row, shard, row, shard, shard, shard, shard, shard, P("fsdp"), P("fsdp"), P(), P()),
        out_specs=(row, row, grad, grad, grad, grad, grad, P(("sp", "fsdp")), P(("sp", "fsdp")), P(), P()),
        check_vma=False,
    )
```

time: 2040 us -> 667 us (0.33)
  waiting for transfers between devices: 1620 us -> 170 us
  starting transfers between devices: 32.5 us -> 79 us
  local copies, waits for them, and re-layouts: 44 us -> 87.9 us
    reduce_scatter x5 -> x4, waiting for transfers between devices: 1150 us -> 1.69 us  [the longest x1 1.69 us: local(): lax.psum_scatter(grad_down, 'fsdp', scatter_dimension=0, tiled=True)]
    all_gather x5 -> x4, waiting for transfers between devices: 440 us -> 0.05 us  [gather_z(): return lax.all_gather(w, 'fsdp', axis=0, tiled=True)]
    ppermute x0 -> x34, waiting for transfers between devices: none -> 152 us  [the longest x32 152 us: swap(): return lax.ppermute(value, 'sp', [(i, i ^ mask) for i in range(count)])]
    ppermute x0 -> x34, starting transfers between devices: none -> 63.3 us  [the longest x32 60.9 us: swap(): return lax.ppermute(value, 'sp', [(i, i ^ mask) for i in range(count)])]
    psum x0 -> x1, blocking collectives: none -> 52.5 us  [local(): tiny = lax.psum(tiny, ('sp', 'fsdp'))]
    unnamed x1 -> x0, blocking collectives: 40.4 us -> none
    dynamic_update_slice x0 -> x17, local copies, waits for them, and re-layouts: none -> 27.5 us  [gather_chunks(): stack = lax.dynamic_update_slice_in_dim(stack, part[None], s ^ mask, 0)]
    unnamed x8 -> x2, other arithmetic: 24.3 us -> 0.24 us
  transfers between devices with their start and end apart: 18 -> 46, of which waited for: 12 -> 25; matrix products, arithmetic and copies ran while one was open for 12% -> 31% of each run, Pallas kernels for 0% -> 0%
where the time goes in v1:
time: 667 us; the launch traced here: 657 us
  matrix products  184 us (28%)
  waiting for transfers between devices  170 us (25%)
  local copies, waits for them, and re-layouts  87.9 us (13%)
  starting transfers between devices  79 us (12%)
  other arithmetic  67.1 us (10%)
  blocking collectives  52.5 us (8%)
  between operations  15.8 us (2%)
    ppermute x32, waiting for transfers between devices, swap(): return lax.ppermute(value, 'sp', [(i, i ^ mask) for i in range(count)])  152 us
    ppermute x32, starting transfers between devices, swap(): return lax.ppermute(value, 'sp', [(i, i ^ mask) for i in range(count)])  60.9 us
    psum x1, blocking collectives, local(): tiny = lax.psum(tiny, ('sp', 'fsdp'))  52.5 us
    dot_general x3, matrix products, times_transposed(): lax.dot_general(a, b, (((1,), (1,)), ((), ())), preferred_element_type=f32)  31.1 us
    dot_general x4, matrix products, over_rows(): lax.dot_general(a, b, (((0,), (0,)), ((), ())), preferred_element_type=f32)  30.8 us
    dynamic_update_slice x17, local copies, waits for them, and re-layouts, gather_chunks(): stack = lax.dynamic_update_slice_in_dim(stack, part[None], s ^ mask, 0)  27.5 us
    dot_general x1, matrix products, attend_back(): jnp.einsum('gqt,td->qgd', grad_s, k, preferred_element_type=f32) * scale  27 us
    dot_general x1, matrix products, attend_back(): jnp.einsum('gqt,qgd->td', grad_s, q, preferred_element_type=f32) * scale  23.8 us
  transfers between devices with their start and end apart: 46, of which 25 were waited for; matrix products, arithmetic and copies ran while one was open for 31% of the time, Pallas kernels for 0%

profile of v1, /device:TPU:0, one launch (start us, length us, event | category | flops | bytes accessed | tf_op | source)
XLA Modules:
  0.0 657.0 jit_solution(212468918248744938)
XLA Ops:
  16.5 11.6 %collective-permute-start = (bf16[256,2048]{1,0:T(8,128)(2,1)S(1)}, bf16[256,2048]{1,0:T(8,128)(2,1)}, u32[]{:S(2)}, u32[]{:S(2)}) collective-permute-start(bf16[256,2048]{1,0:T(8,128)(2,1)S(1)} %bitcast.265), channel_id=1, source_target_pairs={{0,8},{8,0},{16,24},{24,16},{1,9},{9,1},{17,25},{25,17},{2,10},{10... | collective-permute-start | bytes 3145736 | tf_op jit(solution)/shard_map/ppermute | solution.py:72
  44.9 21.8 %collective-permute-done.1 = bf16[256,2048]{1,0:T(8,128)(2,1)} collective-permute-done((bf16[256,2048]{1,0:T(8,128)(2,1)S(1)}, bf16[256,2048]{1,0:T(8,128)(2,1)}, u32[]{:S(2)}, u32[]{:S(2)}) %collective-permute-start.1) | collective-permute-done | bytes 1048608 | tf_op jit(solution)/shard_map/ppermute | solution.py:72
  67.8 16.5 %collective-permute-start.3 = (bf16[128,2048]{1,0:T(8,128)(2,1)S(1)}, bf16[128,2048]{1,0:T(8,128)(2,1)S(1)}, u32[]{:S(2)}, u32[]{:S(2)}) collective-permute-start(bf16[128,2048]{1,0:T(8,128)(2,1)S(1)} %slice.186), channel_id=1, source_target_pairs={{0,8},{8,0},{16,24},{24,16},{1,9},{9,1},{17,25},{25,17},{2,10},{10... | collective-permute-start | bytes 1572872 | tf_op jit(solution)/shard_map/ppermute | solution.py:72
  117.3 16.3 %collective-permute-done.10 = bf16[256,2048]{1,0:T(8,128)(2,1)S(1)} collective-permute-done((bf16[256,2048]{1,0:T(8,128)(2,1)}, bf16[256,2048]{1,0:T(8,128)(2,1)S(1)}, u32[]{:S(2)}, u32[]{:S(2)}) %collective-permute-start.10) | collective-permute-done | bytes 1048608 | tf_op jit(solution)/shard_map/ppermute | solution.py:72
  145.8 7.6 %fusion.108 = (f32[4,1024]{1,0:T(4,128)S(1)}, f32[4,1024,1024]{1,2,0:T(8,128)}) fusion(bf16[1024,4,32]{0,2,1:T(8,128)(2,1)S(1)} %get-tuple-element.39, bf16[1024,4,32]{0,2,1:T(8,128)(2,1)S(1)} %get-tuple-element.38, bf16[1024,32]{0,1:T(8,128)(2,1)S(1)} %get-tuple-element.51, bf16[1024,32]{0,1:T(8,128)(2,1)S(1)} %get-tuple-element.50, ...), kind=kOutput, calls=%fused_computation.228 | convolution fusion | flops 550760448 | bytes 18497536 | tf_op jit(solution)/shard_map/qgd,td->gqt/dot_general | solution.py:41
  153.5 8.0 %fusion.4 = f32[4,1024]{1,0:T(4,128)S(1)} fusion(f32[4,1024,1024]{1,2,0:T(8,128)} %get-tuple-element.61, f32[4,1024]{1,0:T(4,128)S(1)} %get-tuple-element.60), kind=kLoop, calls=%fused_computation.10 | loop fusion | flops 8384512 | bytes 16809984 | tf_op jit(solution)/shard_map/reduce_sum | solution.py:52
  177.8 8.0 %collective-permute-done.5 = bf16[1024,256]{1,0:T(8,128)(2,1)} collective-permute-done((bf16[1024,256]{1,0:T(8,128)(2,1)}, bf16[1024,256]{1,0:T(8,128)(2,1)}, u32[]{:S(2)}, u32[]{:S(2)}) %collective-permute-start.5) | collective-permute-done | bytes 524320 | tf_op jit(solution)/shard_map/ppermute | solution.py:72
  194.9 9.9 %multiply_reduce_fusion = (f32[1024]{0:T(1024)S(1)}, f32[1024,2048]{1,0:T(8,128)}) fusion(bf16[4,256,2048]{2,1,0:T(8,128)(2,1)} %fusion.54, bf16[4,1024,256]{2,1,0:T(8,128)(2,1)S(1)} %fusion.62, bf16[4,256,2048]{2,1,0:T(8,128)(2,1)} %fusion.53), kind=kOutput, calls=%fused_computation.22 | convolution fusion | flops 4303354880 | bytes 18878464 | tf_op jit(solution)/shard_map/dot_general | solution.py:175
  204.8 16.1 %fusion.102 = f32[1024,2048]{1,0:T(8,128)} fusion(bf16[2048,2048]{1,0:T(8,128)(2,1)} %all-gather.9.cloned.1.call-done, f32[1024,2048]{1,0:T(8,128)} %get-tuple-element.63, f32[2048]{0:T(1024)S(1)} %get-tuple-element.15, f32[1024]{0:T(1024)S(1)} %add_rsqrt_fusion), kind=kOutput, calls=%fused_computation.223 | convolution fusion | flops 8596226048 | bytes 25178112 | tf_op jit(solution)/shard_map/dot_general | solution.py:177
  220.9 14.7 %fusion.18 = (bf16[1024,1024]{1,0:T(8,128)(2,1)}, bf16[1024,1024]{1,0:T(8,128)(2,1)}, bf16[1024,1024]{1,0:T(8,128)(2,1)}) fusion(f32[1024,2048]{1,0:T(8,128)} %fusion.102, bf16[1024,2048]{1,0:T(8,128)(2,1)} %bitcast.31, bf16[1024,2048]{1,0:T(8,128)(2,1)} %all-gather.11.cloned.1.call-done), kind=kOutput, calls=%fused_computation.30 | convolution fusion | flops 4311744512 | bytes 23068672 | tf_op jit(solution)/shard_map/dot_general | solution.py:36
  235.6 11.1 %fusion.21 = f32[1024,2048]{1,0:T(8,128)S(1)} fusion(bf16[2048,2048]{1,0:T(8,128)(2,1)S(1)} %copy-done.50, bf16[1024,1024]{1,0:T(8,128)(2,1)} %get-tuple-element.25, bf16[1024,1024]{1,0:T(8,128)(2,1)} %get-tuple-element.24), kind=kOutput, calls=%fused_computation.48 | convolution fusion | flops 8598323200 | bytes 20971520 | tf_op jit(solution)/shard_map/dot_general | solution.py:36
  265.6 7.7 %collective-permute-done.14 = bf16[128,2048]{1,0:T(8,128)(2,1)S(1)} collective-permute-done((bf16[128,2048]{1,0:T(8,128)(2,1)S(1)}, bf16[128,2048]{1,0:T(8,128)(2,1)S(1)}, u32[]{:S(2)}, u32[]{:S(2)}) %collective-permute-start.14) | collective-permute-done | bytes 524320 | tf_op jit(solution)/shard_map/ppermute | solution.py:72
  280.9 14.8 %collective-permute-done.25 = bf16[256,2048]{1,0:T(8,128)(2,1)S(1)} collective-permute-done((bf16[256,2048]{1,0:T(8,128)(2,1)}, bf16[256,2048]{1,0:T(8,128)(2,1)S(1)}, u32[]{:S(2)}, u32[]{:S(2)}) %collective-permute-start.25) | collective-permute-done | bytes 1048608 | tf_op jit(solution)/shard_map/ppermute | solution.py:72
  297.5 17.4 %collective-permute-done.17 = bf16[256,2048]{1,0:T(8,128)(2,1)} collective-permute-done((bf16[256,2048]{1,0:T(8,128)(2,1)}, bf16[256,2048]{1,0:T(8,128)(2,1)}, u32[]{:S(2)}, u32[]{:S(2)}) %collective-permute-start.17) | collective-permute-done | bytes 1048608 | tf_op jit(solution)/shard_map/ppermute | solution.py:72
  348.1 8.1 %fusion.85 = f32[1024,1024,4]{1,0,2:T(8,128)} fusion(bf16[1024,4,64]{0,2,1:T(8,128)(2,1)S(1)} %reshape.378, f32[1024,384]{0,1:T(8,128)S(1)} %fusion.100), kind=kOutput, calls=%fused_computation.185 | convolution fusion | flops 536870912 | bytes 17432576 | tf_op jit(solution)/shard_map/qgd,td->gqt/dot_general | solution.py:62
  356.2 8.4 %fusion.42 = bf16[1024,64]{0,1:T(8,128)(2,1)S(1)} fusion(bf16[1024,4,64]{0,2,1:T(8,128)(2,1)S(1)} %reshape.378, f32[4,1024,1024]{1,2,0:T(8,128)} %get-tuple-element.61, f32[4,1024]{1,0:T(4,128)S(1)} %log_add_fusion), kind=kOutput, calls=%fused_computation.81 | convolution fusion | flops 545325056 | bytes 17448960 | tf_op jit(solution)/shard_map/gqt,qgd->td/dot_general | solution.py:61
  364.7 23.8 %fusion.46 = f32[1024,1,64]{0,2,1:T(8,128)S(1)} fusion(f32[1024,1024,4]{1,0,2:T(8,128)} %fusion.85, f32[4,1024,1024]{1,2,0:T(8,128)} %get-tuple-element.61, f32[4,1024]{1,0:T(4,128)S(1)} %log_add_fusion, pred[1024,1024]{0,1:T(8,128)(4,1)} %fusion.20, bf16[1024,4,32]{0,2,1:T(8,128)(2,1)} %copy-done.25, bf16[1024,4,32]{0,2,1:T(8,128)(2,1)S(1)} %get-tuple-element.38), kind=kOutput, calls=%fused_computation.83 | convolution fusion | flops 567481344 | bytes 35405824 | tf_op jit(solution)/shard_map/gqt,qgd->td/dot_general | solution.py:67
  388.5 27.0 %fusion.34 = f32[1024,4,64]{0,2,1:T(8,128)} fusion(f32[1024,1024,4]{1,0,2:T(8,128)} %fusion.85, f32[4,1024,1024]{1,2,0:T(8,128)} %get-tuple-element.61, f32[4,1024]{1,0:T(4,128)} %copy-done.26, pred[1024,1024]{0,1:T(8,128)(4,1)} %fusion.20, bf16[1024,32]{0,1:T(8,128)(2,1)S(1)} %copy-done.39, bf16[1024,32]{0,1:T(8,128)(2,1)S(1)} %copy-done.37), kind=kOutput, calls=%fused_computation.74 | convolution fusion | flops 567284736 | bytes 35799040 | tf_op jit(solution)/shard_map/gqt,td->qgd/dot_general | solution.py:66
  426.9 15.2 %convolution_convert_fusion = bf16[2048,2048]{1,0:T(8,128)(2,1)} fusion(bf16[1024,1024]{1,0:T(8,128)(2,1)} %get-tuple-element.25, bf16[1024,1024]{1,0:T(8,128)(2,1)} %get-tuple-element.24, f32[1024,2048]{1,0:T(8,128)} %get-tuple-element.63, f32[2048]{0:T(1024)S(1)} %copy-done.33, f32[1024]{0:T(1024)S(1)} %copy-done.48), kind=kOutput, calls=%fused_computation.26 | convolution fusion | flops 8608808960 | bytes 20983808 | tf_op jit(solution)/shard_map/dot_general | solution.py:32
  442.0 8.4 %copy.92 = bf16[4,8,64,2048]{3,2,0,1:T(8,128)(2,1)} copy(bf16[4,8,64,2048]{3,2,1,0:T(8,128)(2,1)} %bitcast.267) | data formatting | bytes 16777216 | tf_op jit(solution)/shard_map/reshape | solution.py:194
  452.6 20.2 %collective-permute-done.31 = bf16[256,2048]{1,0:T(8,128)(2,1)S(1)} collective-permute-done((bf16[256,2048]{1,0:T(8,128)(2,1)}, bf16[256,2048]{1,0:T(8,128)(2,1)S(1)}, u32[]{:S(2)}, u32[]{:S(2)}) %collective-permute-start.31) | collective-permute-done | bytes 1048608 | tf_op jit(solution)/shard_map/ppermute | solution.py:72
  491.3 8.7 %convolution_convert_fusion.1 = bf16[1024,2048]{1,0:T(8,128)(2,1)} fusion(bf16[1024,1024]{1,0:T(8,128)(2,1)S(1)} %copy-done.54, bf16[1024,2048]{1,0:T(8,128)(2,1)} %bitcast.31), kind=kOutput, calls=%fused_computation.39 | convolution fusion | flops 4297064448 | bytes 10485760 | tf_op jit(solution)/shard_map/dot_general | solution.py:32
  511.3 22.4 %collective-permute-done.27 = bf16[2048,384]{1,0:T(8,128)(2,1)} collective-permute-done((bf16[2048,384]{1,0:T(8,128)(2,1)}, bf16[2048,384]{1,0:T(8,128)(2,1)}, u32[]{:S(2)}, u32[]{:S(2)}) %collective-permute-start.27) | collective-permute-done | bytes 1572896 | tf_op jit(solution)/shard_map/ppermute | solution.py:72
  565.4 52.5 %psum.7 = f32[4224]{0:T(1024)S(1)} all-reduce(f32[4224]{0:T(1024)S(1)} %concatenate.101), channel_id=1, replica_groups=mesh['sp'=4,'fsdp'=8] {'sp','fsdp'}, use_global_device_ids=true, to_apply=%region_21.22 | all-reduce | flops 4224 | bytes 33792 | tf_op jit(solution)/shard_map/psum | solution.py:245
  (340 shorter events, 265.1 us)
Async XLA Ops:
  7.2 96.6 %all-gather.7.cloned.1.call-start = ((), (), s32[]{:S(2)}) async-start(), calls=%async_computation.9 | async-start | bytes 1179648 | tf_op jit(solution)/shard_map/all_gather | solution.py:134
  9.8 126.9 %all-gather.5.cloned.1.call-start = ((), (), s32[]{:S(2)}) async-start(), calls=%async_computation.8 | async-start | bytes 2359296 | tf_op jit(solution)/shard_map/all_gather | solution.py:134
  14.1 190.7 %all-gather.9.cloned.1.call-start = ((), (), s32[]{:S(2)}) async-start(), calls=%async_computation.10 | async-start | bytes 9437184 | tf_op jit(solution)/shard_map/all_gather | solution.py:134
  16.5 204.4 %all-gather.11.cloned.1.call-start = ((), (), s32[]{:S(2)}) async-start(), calls=%async_computation.11 | async-start | bytes 4718592 | tf_op jit(solution)/shard_map/all_gather | solution.py:134
  16.5 67.8 %collective-permute-start = (bf16[256,2048]{1,0:T(8,128)(2,1)S(1)}, bf16[256,2048]{1,0:T(8,128)(2,1)}, u32[]{:S(2)}, u32[]{:S(2)}) collective-permute-start(bf16[256,2048]{1,0:T(8,128)(2,1)S(1)} %bitcast.265), channel_id=1, source_target_pairs={{0,8},{8,0},{16,24},{24,16},{1,9},{9,1},{17,25},{25,17},{2,10},{10... | collective-permute-start | bytes 3145736 | tf_op jit(solution)/shard_map/ppermute | solution.py:72
  28.2 38.6 %collective-permute-start.1 = (bf16[256,2048]{1,0:T(8,128)(2,1)S(1)}, bf16[256,2048]{1,0:T(8,128)(2,1)}, u32[]{:S(2)}, u32[]{:S(2)}) collective-permute-start(bf16[256,2048]{1,0:T(8,128)(2,1)S(1)} %bitcast.266), channel_id=1, source_target_pairs={{0,16},{8,24},{16,0},{24,8},{1,17},{9,25},{17,1},{25,9},{2,18},{10... | collective-permute-start | bytes 3145736 | tf_op jit(solution)/shard_map/ppermute | solution.py:72
  31.9 57.0 %collective-permute-start.18 = (bf16[256,2048]{1,0:T(8,128)(2,1)}, bf16[256,2048]{1,0:T(8,128)(2,1)}, u32[]{:S(2)}, u32[]{:S(2)}) collective-permute-start(bf16[256,2048]{1,0:T(8,128)(2,1)} %bitcast.269), channel_id=1, source_target_pairs={{0,8},{8,0},{16,24},{24,16},{1,9},{9,1},{17,25},{25,17},{2,10},{10... | collective-permute-start | bytes 3145736 | tf_op jit(solution)/shard_map/ppermute | solution.py:72
  32.0 54.7 %collective-permute-start.19 = (bf16[256,2048]{1,0:T(8,128)(2,1)}, bf16[256,2048]{1,0:T(8,128)(2,1)}, u32[]{:S(2)}, u32[]{:S(2)}) collective-permute-start(bf16[256,2048]{1,0:T(8,128)(2,1)} %bitcast.270), channel_id=1, source_target_pairs={{0,16},{8,24},{16,0},{24,8},{1,17},{9,25},{17,1},{25,9},{2,18},{10... | collective-permute-start | bytes 3145736 | tf_op jit(solution)/shard_map/ppermute | solution.py:72
  67.8 34.9 %collective-permute-start.3 = (bf16[128,2048]{1,0:T(8,128)(2,1)S(1)}, bf16[128,2048]{1,0:T(8,128)(2,1)S(1)}, u32[]{:S(2)}, u32[]{:S(2)}) collective-permute-start(bf16[128,2048]{1,0:T(8,128)(2,1)S(1)} %slice.186), channel_id=1, source_target_pairs={{0,8},{8,0},{16,24},{24,16},{1,9},{9,1},{17,25},{25,17},{2,10},{10... | collective-permute-start | bytes 1572872 | tf_op jit(solution)/shard_map/ppermute | solution.py:72
  103.9 30.5 %collective-permute-start.9 = (bf16[256,2048]{1,0:T(8,128)(2,1)}, bf16[256,2048]{1,0:T(8,128)(2,1)S(1)}, u32[]{:S(2)}, u32[]{:S(2)}) collective-permute-start(bf16[256,2048]{1,0:T(8,128)(2,1)} %all-gather.7.cloned.1.call-done), channel_id=1, source_target_pairs={{0,8},{8,0},{16,24},{24,16},{1,9},{9,1},{17,25},{25,17},{2,10},{10... | collective-permute-start | bytes 3145736 | tf_op jit(solution)/shard_map/ppermute | solution.py:72
  105.5 28.0 %collective-permute-start.10 = (bf16[256,2048]{1,0:T(8,128)(2,1)}, bf16[256,2048]{1,0:T(8,128)(2,1)S(1)}, u32[]{:S(2)}, u32[]{:S(2)}) collective-permute-start(bf16[256,2048]{1,0:T(8,128)(2,1)} %all-gather.7.cloned.1.call-done), channel_id=1, source_target_pairs={{0,16},{8,24},{16,0},{24,8},{1,17},{9,25},{17,1},{25,9},{2,18},{10... | collective-permute-start | bytes 3145736 | tf_op jit(solution)/shard_map/ppermute | solution.py:72
  134.4 40.6 %collective-permute-start.12 = (bf16[128,2048]{1,0:T(8,128)(2,1)}, bf16[128,2048]{1,0:T(8,128)(2,1)}, u32[]{:S(2)}, u32[]{:S(2)}) collective-permute-start(bf16[128,2048]{1,0:T(8,128)(2,1)} %slice.199), channel_id=1, source_target_pairs={{0,8},{8,0},{16,24},{24,16},{1,9},{9,1},{17,25},{25,17},{2,10},{10... | collective-permute-start | bytes 1572872 | tf_op jit(solution)/shard_map/ppermute | solution.py:72
  135.2 39.8 %collective-permute-start.11 = (bf16[128,2048]{1,0:T(8,128)(2,1)}, bf16[128,2048]{1,0:T(8,128)(2,1)}, u32[]{:S(2)}, u32[]{:S(2)}) collective-permute-start(bf16[128,2048]{1,0:T(8,128)(2,1)} %slice.198), channel_id=1, source_target_pairs={{0,16},{8,24},{16,0},{24,8},{1,17},{9,25},{17,1},{25,9},{2,18},{10... | collective-permute-start | bytes 1572872 | tf_op jit(solution)/shard_map/ppermute | solution.py:72
  262.8 32.9 %collective-permute-start.25 = (bf16[256,2048]{1,0:T(8,128)(2,1)}, bf16[256,2048]{1,0:T(8,128)(2,1)S(1)}, u32[]{:S(2)}, u32[]{:S(2)}) collective-permute-start(bf16[256,2048]{1,0:T(8,128)(2,1)} %pad_maximum_fusion.7), channel_id=1, source_target_pairs={{0,16},{8,24},{16,0},{24,8},{1,17},{9,25},{17,1},{25,9},{2,18},{10... | collective-permute-start | bytes 3145736 | tf_op jit(solution)/shard_map/ppermute | solution.py:72
  264.5 33.0 %collective-permute-start.23 = (bf16[256,2048]{1,0:T(8,128)(2,1)}, bf16[256,2048]{1,0:T(8,128)(2,1)}, u32[]{:S(2)}, u32[]{:S(2)}) collective-permute-start(bf16[256,2048]{1,0:T(8,128)(2,1)} %pad_maximum_fusion.6), channel_id=1, source_target_pairs={{0,8},{8,0},{16,24},{24,16},{1,9},{9,1},{17,25},{25,17},{2,10},{10... | collective-permute-start | bytes 3145736 | tf_op jit(solution)/shard_map/ppermute | solution.py:72
  276.3 38.6 %collective-permute-start.17 = (bf16[256,2048]{1,0:T(8,128)(2,1)}, bf16[256,2048]{1,0:T(8,128)(2,1)}, u32[]{:S(2)}, u32[]{:S(2)}) collective-permute-start(bf16[256,2048]{1,0:T(8,128)(2,1)} %pad_maximum_fusion.5), channel_id=1, source_target_pairs={{0,16},{8,24},{16,0},{24,8},{1,17},{9,25},{17,1},{25,9},{2,18},{10... | collective-permute-start | bytes 3145736 | tf_op jit(solution)/shard_map/ppermute | solution.py:72
  277.7 38.7 %collective-permute-start.15 = (bf16[256,2048]{1,0:T(8,128)(2,1)}, bf16[256,2048]{1,0:T(8,128)(2,1)}, u32[]{:S(2)}, u32[]{:S(2)}) collective-permute-start(bf16[256,2048]{1,0:T(8,128)(2,1)} %pad_maximum_fusion.4), channel_id=1, source_target_pairs={{0,8},{8,0},{16,24},{24,16},{1,9},{9,1},{17,25},{25,17},{2,10},{10... | collective-permute-start | bytes 3145736 | tf_op jit(solution)/shard_map/ppermute | solution.py:72
  339.1 283.0 %reduce-scatter.5.cloned.1.call-start = ((), (), s32[]{:S(2)}) async-start(), calls=%async_computation.12 | async-start | bytes 1769472 | tf_op jit(solution)/shard_map/reduce_scatter | solution.py:196
  426.8 205.2 %reduce-scatter.9.cloned.1.call-start = ((), (), s32[]{:S(2)}) async-start(), calls=%async_computation.14 | async-start | bytes 9437184 | tf_op jit(solution)/shard_map/reduce_scatter | solution.py:196
  450.5 186.8 %reduce-scatter.7.cloned.1.call-start = ((), (), s32[]{:S(2)}) async-start(), calls=%async_computation.13 | async-start | bytes 1179648 | tf_op jit(solution)/shard_map/reduce_scatter | solution.py:218
  452.1 24.2 %collective-permute-start.30 = (bf16[256,2048]{1,0:T(8,128)(2,1)}, bf16[256,2048]{1,0:T(8,128)(2,1)S(1)}, u32[]{:S(2)}, u32[]{:S(2)}) collective-permute-start(bf16[256,2048]{1,0:T(8,128)(2,1)} %get-tuple-element.22), channel_id=1, source_target_pairs={{0,8},{8,0},{16,24},{24,16},{1,9},{9,1},{17,25},{25,17},{2,10},{10... | collective-permute-start | bytes 3145736 | tf_op jit(solution)/shard_map/ppermute | solution.py:72
  491.2 150.6 %reduce-scatter.11.cloned.1.call-start = ((), (), s32[]{:S(2)}) async-start(), calls=%async_computation.15 | async-start | bytes 4718592 | tf_op jit(solution)/shard_map/reduce_scatter | solution.py:186
  502.8 30.9 %collective-permute-start.27 = (bf16[2048,384]{1,0:T(8,128)(2,1)}, bf16[2048,384]{1,0:T(8,128)(2,1)}, u32[]{:S(2)}, u32[]{:S(2)}) collective-permute-start(bf16[2048,384]{1,0:T(8,128)(2,1)} %slice.188), channel_id=1, source_target_pairs={{0,16},{8,24},{16,0},{24,8},{1,17},{9,25},{17,1},{25,9},{2,18},{10... | collective-permute-start | bytes 4718600 | tf_op jit(solution)/shard_map/ppermute | solution.py:72
  502.8 33.0 %collective-permute-start.26 = (bf16[2048,384]{1,0:T(8,128)(2,1)}, bf16[2048,384]{1,0:T(8,128)(2,1)}, u32[]{:S(2)}, u32[]{:S(2)}) collective-permute-start(bf16[2048,384]{1,0:T(8,128)(2,1)} %slice.188), channel_id=1, source_target_pairs={{0,8},{8,0},{16,24},{24,16},{1,9},{9,1},{17,25},{25,17},{2,10},{10... | collective-permute-start | bytes 4718600 | tf_op jit(solution)/shard_map/ppermute | solution.py:72
  (77 other events, 1695.6 us)
Sparse Core Ops, SparseCore 0:
  10.2 43.0 all-gather.6
  55.5 30.0 all-gather.4
  87.8 81.5 all-gather.8
  170.8 45.6 all-gather.10
  426.9 40.1 reduce-scatter.4
  469.2 87.6 reduce-scatter.8
  559.8 30.7 reduce-scatter.6
  592.8 48.9 reduce-scatter.10

commit v2 on v1

v2 whole, which is shorter than its diff:
```python
import functools

import jax
import jax.numpy as jnp
from jax import lax
from jax.experimental import pallas as pl
from jax.experimental.pallas import tpu as pltpu
from jax.sharding import PartitionSpec as P

QUERY_HEADS = 16
KV_HEADS = 4
HD = 64
EPS = 1e-06
BLOCK = 256
VMEM_LIMIT = 60 << 20
MESH = pl.DeviceIdType.MESH
f32 = jnp.float32
bf16 = jnp.bfloat16


def params(collective=None, grid=0):
    return pltpu.CompilerParams(
        dimension_semantics=("arbitrary",) * grid if grid else None,
        vmem_limit_bytes=VMEM_LIMIT,
        collective_id=collective,
        has_side_effects=collective is not None,
    )


def cost(micros):
    return pl.CostEstimate(flops=0, bytes_accessed=int(micros * 3_600_000), transcendentals=0)


ANY = pl.BlockSpec(memory_space=pl.ANY)
VMEM = pl.BlockSpec(memory_space=pltpu.VMEM)
DMA = pltpu.SemaphoreType.DMA


def shape(dims, dtype=bf16):
    return jax.ShapeDtypeStruct(dims, dtype)


def dot(a, b):
    return jnp.dot(a, b, preferred_element_type=f32)


def dot_nt(a, b):
    return lax.dot_general(a, b, (((1,), (1,)), ((), ())), preferred_element_type=f32)


def greet(S, sibling):
    s, f = lax.axis_index("sp"), lax.axis_index("fsdp")
    barrier = pltpu.get_barrier_semaphore()
    for k in range(1, S):
        pl.semaphore_signal(barrier, inc=1, device_id={"sp": lax.rem(s + k, S)}, device_id_type=MESH)
    if sibling:
        pl.semaphore_signal(barrier, inc=1, device_id={"fsdp": f + 1 - 2 * lax.rem(f, 2)}, device_id_type=MESH)
    pl.semaphore_wait(barrier, S - 1 + int(sibling))


def to_peer(src, dst, send, recv, k, S):
    s = lax.axis_index("sp")
    return pltpu.make_async_remote_copy(
        src_ref=src, dst_ref=dst, send_sem=send, recv_sem=recv, device_id={"sp": lax.rem(s + k, S)}, device_id_type=MESH
    )


def mates(s):
    return s + 1 - 2 * lax.rem(s, 2), lax.rem(s + 2, 4), 3 - s


def push(src, dst, send, recv, where):
    return pltpu.make_async_remote_copy(
        src_ref=src, dst_ref=dst, send_sem=send, recv_sem=recv, device_id=where, device_id_type=MESH
    )


class Gather:
    def __init__(self, S, src, dst, sems, halves=False, inner=False):
        self.S, self.src, self.halves = S, src, halves
        self.slot = (lambda j: dst.at[:, j]) if inner else (lambda j: dst.at[j])
        self.send, self.recv, self.own, self.stage = sems[:4]
        self.swap_send, self.swap_recv = sems[4:] if halves else (None, None)
        self.s, self.f = lax.axis_index("sp"), lax.axis_index("fsdp")
        self.rows = src.shape[0] // (2 if halves else 1)
        self.size = self.rows // 2 if S == 4 else self.rows

    @staticmethod
    def sems(S, chunk, halves=False):
        count = 6 if S == 4 else S - 1
        base = [DMA((count,)), DMA((count,)), DMA((2,)), pltpu.VMEM(chunk.shape, chunk.dtype)]
        return base + [DMA((S - 1,)), DMA((S - 1,))] if halves else base

    def base(self, mine=True):
        if not self.halves:
            return 0
        core = lax.rem(self.f, 2)
        return (core if mine else 1 - core) * self.rows

    def piece(self, ref, n):
        return ref.at[pl.ds(self.base() + n * self.size, self.size)]

    def share(self, slot, mine):
        if not self.halves:
            return self.slot(slot)
        return self.slot(slot).at[pl.ds(self.base(mine), self.rows)]

    def steps(self):
        s, S = self.s, self.S
        if S != 4:
            return [(self.src, s, lax.rem(s + S - k, S), 0, lax.rem(s + k, S)) for k in range(1, S)]
        x, y, d = mates(s)
        return [
            (self.src, s, x, 0, x),
            (self.src, s, y, 1, y),
            (self.src, s, x, 1, x),
            (self.src, s, y, 0, y),
            (self.slot(x), x, d, 0, y),
            (self.slot(y), y, d, 1, x),
        ]

    def copy(self, n, here):
        src, there, lands, piece, target = self.steps()[n]
        slot = lands if here else there
        return push(
            self.piece(src, piece), self.piece(self.slot(slot), piece), self.send.at[n], self.recv.at[n], {"sp": target}
        )

    def passing(self, n, mine):
        slots = mates(self.s) if self.S == 4 else [lax.rem(self.s + self.S - k, self.S) for k in range(1, self.S)]
        sibling = {"fsdp": self.f + 1 - 2 * lax.rem(self.f, 2)}
        return push(
            self.share(slots[n], True), self.share(slots[n], mine), self.swap_send.at[n], self.swap_recv.at[n], sibling
        )

    def local(self, out):
        if out:
            return pltpu.make_async_copy(self.stage, self.slot(self.s), self.own.at[1])
        return pltpu.make_async_copy(self.src, self.stage, self.own.at[0])

    def start(self):
        for n in range(4 if self.S == 4 else self.S - 1):
            self.copy(n, False).start()
        self.local(False).start()

    def finish(self):
        self.local(False).wait()
        self.local(True).start()
        waits = {0: 4, 1: 5} if self.S == 4 else {}
        ready = {2: 0, 3: 1, 5: 2} if self.S == 4 else {n: n for n in range(self.S - 1)}
        for n in range(len(self.steps())):
            self.copy(n, True).wait_recv()
            if n in waits:
                self.copy(waits[n], False).start()
            if self.halves and n in ready:
                self.passing(ready[n], True).start()
        self.local(True).wait()
        for n in range(len(self.steps())):
            self.copy(n, False).wait_send()
        if self.halves:
            for n in range(self.S - 1):
                self.passing(n, True).wait_send()
                self.passing(n, False).wait_recv()


def gather_kernel(S, src, dst, *sems):
    greet(S, False)
    move = Gather(S, src, dst, sems)
    move.start()
    move.finish()


def gather_sp(S, x, collective):
    return pl.pallas_call(
        functools.partial(gather_kernel, S),
        in_specs=[ANY],
        out_specs=ANY,
        out_shape=shape((S,) + x.shape, x.dtype),
        scratch_shapes=Gather.sems(S, x),
        compiler_params=params(collective),
        cost_estimate=cost(45),
    )(x)


def forward_kernel(S, heads, x_ref, g_ref, w_ref, pos_ref, cos_ref, sin_ref, gq_ref, gk_ref, wout_ref, normed_t_ref, raw_ref, rot_ref, lse_ref, mix_t_ref, mix_all, wout_all, k_buf, vt_buf, mix_buf, mix_send, mix_recv, mix_own, *sems):
    i = pl.program_id(0)
    s = lax.axis_index("sp")
    qw = heads * HD
    half = HD // 2
    move = Gather(S, wout_ref, wout_all, sems, halves=True, inner=True)

    @pl.when(i == 0)
    def _():
        greet(S, True)
        move.start()

    x = x_ref[...].astype(f32)
    scale = lax.rsqrt(jnp.mean(x * x, axis=-1, keepdims=True) + EPS)
    scaled = x * scale * g_ref[...]
    normed = scaled.astype(bf16)
    normed_t_ref[...] = scaled.T.astype(bf16)
    raw = dot(normed, w_ref[...]).T
    raw_ref[...] = raw
    cosine, sine = cos_ref[...], sin_ref[...]

    def prep(u, gain):
        n = u * lax.rsqrt(jnp.mean(u * u, axis=0, keepdims=True) + EPS) * gain
        front, back = n[:half], n[half:]
        return jnp.concatenate([front * cosine - back * sine, back * cosine + front * sine], axis=0)

    q = [prep(raw[h * HD : (h + 1) * HD], gq_ref[...]).astype(bf16) for h in range(heads)]
    kt = prep(raw[qw : qw + HD], gk_ref[...])
    vt = raw[qw + HD :].astype(bf16)
    rot_ref[...] = jnp.concatenate(q + [kt.astype(bf16), vt], axis=0)
    blocks = pl.num_programs(0)
    steps = mix_buf.shape[0]

    x_mate, y_mate, d_mate = mates(s)

    def mix_copy(block, k, here):
        rows = pl.ds(block * BLOCK, BLOCK)
        n = block * (S - 1) + k - 1
        if S != 4:
            slot = lax.rem(s + S - k, S) if here else s
            return push(mix_buf.at[block], mix_all.at[slot, rows], mix_send.at[n], mix_recv.at[n], {"sp": lax.rem(s + k, S)})
        if k < 3:
            mate = x_mate if k == 1 else y_mate
            slot = mate if here else s
            return push(mix_buf.at[block], mix_all.at[slot, rows], mix_send.at[n], mix_recv.at[n], {"sp": mate})
        source, mate = (x_mate, y_mate) if block < steps // 2 else (y_mate, x_mate)
        slot = d_mate if here else source
        return push(mix_all.at[source, rows], mix_all.at[slot, rows], mix_send.at[n], mix_recv.at[n], {"sp": mate})

    def mix_local(block):
        return pltpu.make_async_copy(mix_buf.at[block], mix_all.at[s, pl.ds(block * BLOCK, BLOCK)], mix_own.at[block])

    for step in range(steps):

        @pl.when(i == step)
        def _():
            n = (step + 1) * BLOCK
            k_buf[step * BLOCK : n, :] = kt.T.astype(bf16)
            vt_buf[:, step * BLOCK : n] = vt
            col = lax.broadcasted_iota(jnp.int32, (n, BLOCK), 0)
            row = step * BLOCK + lax.broadcasted_iota(jnp.int32, (n, BLOCK), 1)
            bias = jnp.where((col <= row) & (row - col <= pos_ref[...]), 0.0, -1e30)
            keys, values = k_buf[:n, :], vt_buf[:, :n]
            mixes, lses = [], []
            for h in range(heads):
                e = jnp.exp(dot(keys, q[h] * 0.125) + bias)
                total = jnp.sum(e, axis=0, keepdims=True)
                p = (e * (1.0 / total)).astype(bf16)
                mixes.append(dot(values, p))
                lses.append(jnp.log(total))
            mix = jnp.concatenate(mixes, axis=0)
            mix_t_ref[...] = mix.astype(bf16)
            lse_ref[...] = jnp.concatenate(lses + [jnp.zeros((8 - heads, BLOCK), f32)], axis=0)
            mix_buf[step] = mix.T.astype(bf16)
            for k in range(1, 3 if S == 4 else S):
                mix_copy(step, k, False).start()
            mix_local(step).start()

    @pl.when(i == blocks - 1)
    def _():
        for block in range(steps):
            for k in range(1, 3 if S == 4 else S):
                mix_copy(block, k, True).wait_recv()
                if S == 4 and k == (1 if block < steps // 2 else 2):
                    mix_copy(block, 3, False).start()
        for block in range(steps):
            if S == 4:
                mix_copy(block, 3, True).wait_recv()
            for k in range(1, S):
                mix_copy(block, k, False).wait_send()
            mix_local(block).wait()
        move.finish()


def forward_attention(S, x, gain, w, pos, cosine, sine, gain_q, gain_k, wout, heads, collective):
    length, width = x.shape
    hw = w.shape[1]
    qw = heads * HD
    steps = length // BLOCK
    full = lambda i: (0, 0)
    rows = lambda i: (i, 0)
    cols = lambda i: (0, i)
    return pl.pallas_call(
        functools.partial(forward_kernel, S, heads),
        grid=(steps,),
        in_specs=[
            pl.BlockSpec((BLOCK, width), rows),
            pl.BlockSpec((1, width), full),
            pl.BlockSpec((width, hw), full),
            pl.BlockSpec((1, BLOCK), cols),
            pl.BlockSpec((HD // 2, BLOCK), cols),
            pl.BlockSpec((HD // 2, BLOCK), cols),
            pl.BlockSpec((HD, 1), full),
            pl.BlockSpec((HD, 1), full),
            ANY,
        ],
        out_specs=[
            pl.BlockSpec((width, BLOCK), cols),
            pl.BlockSpec((hw, BLOCK), cols),
            pl.BlockSpec((hw, BLOCK), cols),
            pl.BlockSpec((8, BLOCK), cols),
            pl.BlockSpec((qw, BLOCK), cols),
            ANY,
            ANY,
        ],
        out_shape=[
            shape((width, length)),
            shape((hw, length), f32),
            shape((hw, length)),
            shape((8, length), f32),
            shape((qw, length)),
            shape((S, length, qw)),
            shape((wout.shape[0], S) + wout.shape[1:]),
        ],
        scratch_shapes=[
            pltpu.VMEM((length, HD), bf16),
            pltpu.VMEM((HD, length), bf16),
            pltpu.VMEM((steps, BLOCK, qw), bf16),
            DMA((steps * (S - 1),)),
            DMA((steps * (S - 1),)),
            DMA((steps,)),
        ]
        + Gather.sems(S, wout, True),
        compiler_params=params(collective, 1),
        cost_estimate=cost(45),
    )(x, gain, w, pos, cosine, sine, gain_q, gain_k, wout)


def middle_kernel(S, T, x_ref, mix_ref, wout_ref, g_ref, ct_ref, mid_ref, ffn_ref, ffn_t_ref, ct_all, *sems):
    i = pl.program_id(0)
    s = lax.axis_index("sp")
    move = Gather(S, ct_ref, ct_all, sems)

    @pl.when(i == 0)
    def _():
        greet(S, False)
        move.start()

    middle = x_ref[...].astype(f32)
    total = dot(mix_ref[0], wout_ref[0])
    for j in range(1, S):
        total += dot(mix_ref[j], wout_ref[j])
    middle = middle + total

    @pl.when(i == s)
    def _():
        mid_ref[...] = middle

    scaled = middle * lax.rsqrt(jnp.mean(middle * middle, axis=-1, keepdims=True) + EPS) * g_ref[...]
    ffn_ref[...] = scaled.astype(bf16)
    ffn_t_ref[...] = scaled.T.astype(bf16)

    @pl.when(i == pl.num_programs(0) - 1)
    def _():
        move.finish()


def middle_rows(S, x, mix_all, wout_all, gain, ct, collective):
    length, width = x.shape
    T = length // S
    qw = mix_all.shape[2]
    return pl.pallas_call(
        functools.partial(middle_kernel, S, T),
        grid=(S,),
        in_specs=[
            pl.BlockSpec((T, width), lambda i: (i, 0)),
            pl.BlockSpec((S, T, qw), lambda i: (0, i, 0)),
            pl.BlockSpec((S, qw, width), lambda i: (0, 0, 0)),
            pl.BlockSpec((1, width), lambda i: (0, 0)),
            ANY,
        ],
        out_specs=[
            pl.BlockSpec((T, width), lambda i: (0, 0)),
            pl.BlockSpec((T, width), lambda i: (i, 0)),
            pl.BlockSpec((width, T), lambda i: (0, i)),
            ANY,
        ],
        out_shape=[shape((T, width), f32), shape((length, width)), shape((width, length)), shape((S, T, width))],
        scratch_shapes=Gather.sems(S, ct),
        compiler_params=params(collective, 1),
        cost_estimate=cost(45),
    )(x, mix_all, wout_all, gain, ct)


def ffn_kernel(S, ffn_ref, ct_ref, wg_ref, wu_ref, wqkv_ref, gate_ref, up_ref, hid_ref, down_ref, wqkv_all, *sems):
    i = pl.program_id(0)
    move = Gather(S, wqkv_ref, wqkv_all, sems, halves=True)

    @pl.when(i == 0)
    def _():
        greet(S, True)
        move.start()

    rows = ffn_ref[...]
    gate, up = dot(rows, wg_ref[...]), dot(rows, wu_ref[...])
    gate_ref[...] = gate
    up_ref[...] = up
    hidden = gate / (1.0 + jnp.exp(-gate)) * up
    hid_ref[...] = hidden.astype(bf16)
    down_ref[...] = dot(hidden.T.astype(bf16), ct_ref[...]).astype(bf16)

    @pl.when(i == pl.num_programs(0) - 1)
    def _():
        move.finish()


def ffn_forward(S, ffn_in, ct_all, w_gu, wqkv_s, collective):
    length, width = ffn_in.shape
    FFs = w_gu.shape[1] // 2
    tiles = FFs // BLOCK
    whole = lambda i: (0, 0)
    return pl.pallas_call(
        functools.partial(ffn_kernel, S),
        grid=(tiles,),
        in_specs=[
            pl.BlockSpec((length, width), whole),
            pl.BlockSpec((length, width), whole),
            pl.BlockSpec((width, BLOCK), lambda i: (0, i)),
            pl.BlockSpec((width, BLOCK), lambda i: (0, tiles + i)),
            ANY,
        ],
        out_specs=[
            pl.BlockSpec((length, BLOCK), lambda i: (0, i)),
            pl.BlockSpec((length, BLOCK), lambda i: (0, i)),
            pl.BlockSpec((length, BLOCK), lambda i: (0, i)),
            pl.BlockSpec((BLOCK, width), lambda i: (i, 0)),
            ANY,
        ],
        out_shape=[
            shape((length, FFs), f32),
            shape((length, FFs), f32),
            shape((length, FFs)),
            shape((FFs, width)),
            shape((S,) + wqkv_s.shape),
        ],
        scratch_shapes=Gather.sems(S, wqkv_s, True),
        compiler_params=params(collective, 1),
        cost_estimate=cost(20),
    )(ffn_in, ct_all, w_gu, w_gu, wqkv_s)


def ffn_back_kernel(S, F, ct_ref, wd_ref, gate_ref, up_ref, ffn_t_ref, dgu_ref, pgu_ref):
    gh = dot_nt(ct_ref[...], wd_ref[...])
    gate, up = gate_ref[...], up_ref[...]
    sig = 1.0 / (1.0 + jnp.exp(-gate))
    d_gate = (gh * up * sig * (1.0 + gate * (1.0 - sig))).astype(bf16)
    d_up = (gh * (gate * sig)).astype(bf16)
    dgu_ref[0] = d_gate
    dgu_ref[1] = d_up
    ffn_t = ffn_t_ref[...]
    rows = pgu_ref.shape[3]
    for n, d in enumerate((d_gate, d_up)):
        part = dot(ffn_t, d).astype(bf16)
        for j in range(S):
            for m in range(F):
                pgu_ref[m, j, n] = part[(j * F + m) * rows : (j * F + m + 1) * rows]


def ffn_backward(S, F, ct_all, w_dn, gate, up, ffn_t):
    length, FFs = gate.shape
    width = ct_all.shape[1]
    tiles = FFs // BLOCK
    rows = width // (S * F)
    whole = lambda i: (0, 0)
    col = lambda i: (0, i)
    return pl.pallas_call(
        functools.partial(ffn_back_kernel, S, F),
        grid=(tiles,),
        in_specs=[
            pl.BlockSpec((length, width), whole),
            pl.BlockSpec((BLOCK, width), lambda i: (i, 0)),
            pl.BlockSpec((length, BLOCK), col),
            pl.BlockSpec((length, BLOCK), col),
            pl.BlockSpec((width, length), whole),
        ],
        out_specs=[
            pl.BlockSpec((2, length, BLOCK), lambda i: (0, 0, i)),
            pl.BlockSpec((F, S, 2, rows, BLOCK), lambda i: (0, 0, 0, 0, i)),
        ],
        out_shape=[shape((2, length, FFs)), shape((F, S, 2, rows, FFs))],
        compiler_params=params(None, 1),
        cost_estimate=cost(1),
    )(ct_all, w_dn, gate, up, ffn_t)


def sum_over_sp(S, compute, acc, send_buf, recv_buf, send, recv):
    s = lax.axis_index("sp")
    if S != 4:

        def copy(k):
            return push(
                send_buf.at[k - 1], recv_buf.at[k - 1], send.at[k - 1], recv.at[k - 1], {"sp": lax.rem(s + k, S)}
            )

        for k in range(1, S):
            compute(lax.rem(s + k, S), send_buf.at[k - 1])
            copy(k).start()
        compute(s, acc)
        for k in range(1, S):
            copy(k).wait_recv()
            acc[...] += recv_buf[k - 1].astype(f32)
        return [copy(k) for k in range(1, S)]

    x, y, d = mates(s)
    half = acc.shape[0] // 2
    low, high = pl.ds(0, half), pl.ds(half, half)

    def copy(n):
        buf, rows, target = [(0, low, y), (0, high, x), (1, high, x), (2, low, y), (1, low, x), (2, high, y)][n]
        return push(send_buf.at[buf, rows], recv_buf.at[buf, rows], send.at[n], recv.at[n], {"sp": target})

    compute(d, send_buf.at[0])
    copy(0).start()
    copy(1).start()
    compute(x, send_buf.at[1])
    copy(2).start()
    compute(y, send_buf.at[2])
    copy(3).start()
    copy(0).wait_recv()
    send_buf[1, :half] = (send_buf[1, :half].astype(f32) + recv_buf[0, :half].astype(f32)).astype(bf16)
    copy(4).start()
    copy(1).wait_recv()
    send_buf[2, half:] = (send_buf[2, half:].astype(f32) + recv_buf[0, half:].astype(f32)).astype(bf16)
    copy(5).start()
    compute(s, acc)
    for n in range(2, 6):
        copy(n).wait_recv()
    acc[...] += recv_buf[1].astype(f32) + recv_buf[2].astype(f32)
    return [copy(n) for n in range(6)]


def middle_back_kernel(S, dgu_ref, wgu_ref, wout_ref, mid_ref, g_ref, ct_ref, gm_ref, dattn_ref, gg_ref, dmix_ref, acc, send_buf, recv_buf, mix_buf, send, recv, mix_send, mix_recv, mix_own):
    s = lax.axis_index("sp")
    T, width = mid_ref.shape
    FFs = dgu_ref.shape[2]
    tile = 512
    greet(S, False)

    def compute(chunk, out):
        rows = pl.ds(pl.multiple_of(chunk * T, T), T)
        d_gate, d_up = dgu_ref[0, rows, :], dgu_ref[1, rows, :]
        for c in range(0, width, tile):
            part = dot_nt(d_gate, wgu_ref[c : c + tile, :FFs]) + dot_nt(d_up, wgu_ref[c : c + tile, FFs:])
            out[:, c : c + tile] = part.astype(out.dtype)

    copies = sum_over_sp(S, compute, acc, send_buf, recv_buf, send, recv)
    v, e = mid_ref[...], acc[...]
    r = lax.rsqrt(jnp.mean(v * v, axis=-1, keepdims=True) + EPS)
    gg_ref[...] = jnp.sum(e * v * r, axis=0, keepdims=True)
    ge = g_ref[...] * e
    gm = ct_ref[...].astype(f32) + r * ge - v * (r * r * r * jnp.mean(ge * v, axis=-1, keepdims=True))
    gm_ref[...] = gm
    d_attn = gm.astype(bf16)
    dattn_ref[...] = d_attn

    def mix_copy(k, slot):
        rows = pl.ds(pl.multiple_of(slot * T, T), T)
        return to_peer(mix_buf.at[k], dmix_ref.at[rows], mix_send.at[k - 1], mix_recv.at[k - 1], k, S)

    for k in range(1, S):
        mix_buf[k] = dot_nt(d_attn, wout_ref[lax.rem(s + k, S)]).astype(bf16)
        mix_copy(k, s).start()
    mix_buf[0] = dot_nt(d_attn, wout_ref[s]).astype(bf16)
    own = pltpu.make_async_copy(mix_buf.at[0], dmix_ref.at[pl.ds(pl.multiple_of(s * T, T), T)], mix_own)
    own.start()
    for copy in copies:
        copy.wait_send()
    for k in range(1, S):
        mix_copy(k, s).wait_send()
        mix_copy(k, lax.rem(s + S - k, S)).wait_recv()
    own.wait()


def middle_back(S, dgu, w_gu, wout_all, mid, gain, ct, collective):
    T, width = mid.shape
    qw = wout_all.shape[1]
    return pl.pallas_call(
        functools.partial(middle_back_kernel, S),
        in_specs=[VMEM] * 6,
        out_specs=[VMEM, VMEM, VMEM, ANY],
        out_shape=[shape((T, width), f32), shape((T, width)), shape((1, width), f32), shape((S * T, qw))],
        scratch_shapes=[
            pltpu.VMEM((T, width), f32),
            pltpu.VMEM((S - 1, T, width), bf16),
            pltpu.VMEM((S - 1, T, width), bf16),
            pltpu.VMEM((S, T, qw), bf16),
            DMA((max(6, S - 1),)),
            DMA((max(6, S - 1),)),
            DMA((S - 1,)),
            DMA((S - 1,)),
            DMA,
        ],
        compiler_params=params(collective),
        cost_estimate=cost(1),
    )(dgu, w_gu, wout_all, mid, gain, ct)


def attn_back_kernel(S, heads, dmix_ref, rot_ref, raw_ref, lse_ref, pos_ref, cos_ref, sin_ref, gq_ref, gk_ref, dattn_ref, dproj_ref, gg_ref, dattn_all, k_buf, v_buf, dk_acc, dv_acc, *sems):
    i = pl.program_id(0)
    qw = heads * HD
    half = HD // 2
    length = rot_ref.shape[1]
    move = Gather(S, dattn_ref, dattn_all, sems)

    @pl.when(i == 0)
    def _():
        greet(S, False)
        move.start()
        k_buf[...] = rot_ref[qw : qw + HD, :].astype(f32).T.astype(bf16)
        v_buf[...] = rot_ref[qw + HD :, :].astype(f32).T.astype(bf16)
        dk_acc[...] = jnp.zeros_like(dk_acc)
        dv_acc[...] = jnp.zeros_like(dv_acc)
        gg_ref[...] = jnp.zeros_like(gg_ref)

    def unprep(e, u, gain, cosine, sine):
        front, back = e[:half], e[half:]
        e = jnp.concatenate([front * cosine + back * sine, back * cosine - front * sine], axis=0)
        r = lax.rsqrt(jnp.mean(u * u, axis=0, keepdims=True) + EPS)
        ge = gain * e
        du = r * ge - u * (r * r * r * jnp.mean(ge * u, axis=0, keepdims=True))
        return du, jnp.sum(e * u * r, axis=1, keepdims=True)

    for step in range(length // BLOCK):

        @pl.when(i == step)
        def _():
            n = (step + 1) * BLOCK
            here = slice(step * BLOCK, n)
            col = lax.broadcasted_iota(jnp.int32, (n, BLOCK), 0)
            row = step * BLOCK + lax.broadcasted_iota(jnp.int32, (n, BLOCK), 1)
            bias = jnp.where((col <= row) & (row - col <= pos_ref[:, here]), 0.0, -1e30)
            keys, values = k_buf[:n, :], v_buf[:n, :]
            kt = rot_ref[qw : qw + HD, :n]
            dmix = dmix_ref[...]
            dmix_t = dmix.astype(f32).T.astype(bf16)
            qt = rot_ref[:qw, here]
            q = qt.astype(f32).T.astype(bf16)
            cosine, sine = cos_ref[:, here], sin_ref[:, here]
            dqs, gain_sum = [], jnp.zeros((HD, 1), f32)
            dk, dv = jnp.zeros((n, HD), f32), jnp.zeros((n, HD), f32)
            for h in range(heads):
                part = slice(h * HD, (h + 1) * HD)
                p = jnp.exp(dot(keys, qt[part] * 0.125) + bias - lse_ref[h : h + 1, here])
                dv += dot(p.astype(bf16), dmix[:, part])
                dp = dot(values, dmix_t[part])
                inner = jnp.sum(dp * p, axis=0, keepdims=True)
                ds = (p * (dp - inner)).astype(bf16)
                dk += dot(ds, q[:, part])
                dq = (dot(kt, ds) * 0.125).astype(bf16).astype(f32)
                du, dg = unprep(dq, raw_ref[part, here], gq_ref[...], cosine, sine)
                dqs.append(du)
                gain_sum += dg
            dk_acc[:n, :] += dk
            dv_acc[:n, :] += dv
            gg_ref[:, :1] += gain_sum
            dproj_ref[here, :qw] = jnp.concatenate(dqs, axis=0).T.astype(bf16)

    @pl.when(i == pl.num_programs(0) - 1)
    def _():
        dk = (dk_acc[...] * 0.125).astype(bf16).astype(f32).T
        du, dg = unprep(dk, raw_ref[qw : qw + HD, :], gk_ref[...], cos_ref[...], sin_ref[...])
        gg_ref[:, 1:2] += dg
        dproj_ref[:, qw:] = jnp.concatenate([du.T, dv_acc[...].astype(bf16).astype(f32)], axis=1).astype(bf16)
        move.finish()


def attention_back(S, dmix, rot, raw, lse, pos, cosine, sine, gain_q, gain_k, d_attn, heads, collective):
    length = dmix.shape[0]
    hw = rot.shape[0]
    whole = lambda a: pl.BlockSpec(a.shape, lambda i: (0, 0))
    return pl.pallas_call(
        functools.partial(attn_back_kernel, S, heads),
        grid=(length // BLOCK,),
        in_specs=[pl.BlockSpec((BLOCK, heads * HD), lambda i: (i, 0))]
        + [whole(a) for a in (rot, raw, lse, pos, cosine, sine, gain_q, gain_k)]
        + [ANY],
        out_specs=[pl.BlockSpec((length, hw), lambda i: (0, 0)), pl.BlockSpec((HD, 128), lambda i: (0, 0)), ANY],
        out_shape=[shape((length, hw)), shape((HD, 128), f32), shape((S,) + d_attn.shape)],
        scratch_shapes=[
            pltpu.VMEM((length, HD), bf16),
            pltpu.VMEM((length, HD), bf16),
            pltpu.VMEM((length, HD), f32),
            pltpu.VMEM((length, HD), f32),
        ]
        + Gather.sems(S, d_attn),
        compiler_params=params(collective, 1),
        cost_estimate=cost(1),
    )(dmix, rot, raw, lse, pos, cosine, sine, gain_q, gain_k, d_attn)


def input_back_kernel(S, dproj_ref, dproj_hbm, mix_t_ref, dattn_ref, normed_t_ref, wqkv_ref, x_ref, g_ref, gm_ref, pout_ref, pqkv_ref, gin_ref, gg_ref, got, send, recv):
    s = lax.axis_index("sp")
    T, width = x_ref.shape
    greet(S, False)

    def copy(k, slot):
        rows = pl.ds(pl.multiple_of(lax.rem(s + k, S) * T, T), T)
        return to_peer(dproj_hbm.at[rows], got.at[slot], send.at[k - 1], recv.at[k - 1], k, S)

    for k in range(1, S):
        copy(k, s).start()
    tile = 512
    mix_t, dproj = mix_t_ref[...], dproj_ref[...]
    for c in range(0, width, tile):
        pout_ref[:, c : c + tile] = dot(mix_t, dattn_ref[:, c : c + tile]).astype(bf16)
    for c in range(0, width, tile):
        pqkv_ref[c : c + tile, :] = dot(normed_t_ref[c : c + tile, :], dproj).astype(bf16)
    e = dot_nt(dproj_ref[pl.ds(pl.multiple_of(s * T, T), T), :], wqkv_ref[s])
    for k in range(1, S):
        slot = lax.rem(s + S - k, S)
        copy(k, slot).wait_recv()
        e += dot_nt(got[slot], wqkv_ref[slot])
    v = x_ref[...].astype(f32)
    r = lax.rsqrt(jnp.mean(v * v, axis=-1, keepdims=True) + EPS)
    gg_ref[...] = jnp.sum(e * v * r, axis=0, keepdims=True)
    ge = g_ref[...] * e
    gin_ref[...] = gm_ref[...] + r * ge - v * (r * r * r * jnp.mean(ge * v, axis=-1, keepdims=True))
    for k in range(1, S):
        copy(k, s).wait_send()


def input_back(S, dproj, mix_t, dattn_all, normed_t, wqkv_all, x, gain, gm, collective):
    T, width = x.shape
    hw = dproj.shape[1]
    return pl.pallas_call(
        functools.partial(input_back_kernel, S),
        in_specs=[VMEM, ANY] + [VMEM] * 7,
        out_specs=[VMEM] * 4,
        out_shape=[shape((mix_t.shape[0], width)), shape((width, hw)), shape((T, width), f32), shape((1, width), f32)],
        scratch_shapes=[pltpu.VMEM((S, T, hw), bf16), DMA((S - 1,)), DMA((S - 1,))],
        compiler_params=params(collective),
        cost_estimate=cost(1),
    )(dproj, dproj, mix_t, dattn_all, normed_t, wqkv_all, x, gain, gm)


def output_kernel(S, hid_ref, wd_ref, mid_ref, out_ref, acc, send_buf, recv_buf, send, recv):
    s = lax.axis_index("sp")
    T, width = mid_ref.shape
    tile = 512
    greet(S, False)

    def compute(chunk, out):
        rows = hid_ref[pl.ds(pl.multiple_of(chunk * T, T), T), :]
        for c in range(0, width, tile):
            out[:, c : c + tile] = dot(rows, wd_ref[:, c : c + tile]).astype(out.dtype)

    copies = sum_over_sp(S, compute, acc, send_buf, recv_buf, send, recv)
    out_ref[...] = (mid_ref[...] + acc[...]).astype(bf16)
    for copy in copies:
        copy.wait_send()


def output_rows(S, hidden, w_dn, mid, collective):
    T, width = mid.shape
    return pl.pallas_call(
        functools.partial(output_kernel, S),
        in_specs=[VMEM] * 3,
        out_specs=VMEM,
        out_shape=shape((T, width)),
        scratch_shapes=[
            pltpu.VMEM((T, width), f32),
            pltpu.VMEM((S - 1, T, width), bf16),
            pltpu.VMEM((S - 1, T, width), bf16),
            DMA((max(6, S - 1),)),
            DMA((max(6, S - 1),)),
        ],
        compiler_params=params(collective),
        cost_estimate=cost(40),
    )(hidden, w_dn, mid)


def ordered(value, *after):
    return lax.optimization_barrier((value,) + after)[0]


def local(x_own, positions, ct_own, w_qkv, w_out, w_gate, w_up, w_down, gain_attn, gain_ffn, gain_query, gain_key):
    S, F = lax.axis_size("sp"), lax.axis_size("fsdp")
    s = lax.axis_index("sp")
    _, T, D = x_own.shape
    L = positions.shape[1]
    copies = max(1, S // KV_HEADS)
    QW = QUERY_HEADS * HD
    KW = KV_HEADS * HD
    heads = QUERY_HEADS // S
    qw = heads * HD
    hw = qw + 2 * HD
    FF = w_gate.shape[1]
    FFs = FF // S
    rows_d = D // (S * F)
    rows_o = QW // (S * F)
    x_own = x_own[0]
    ct_own = ct_own[0]

    def cut(w, start, size, axis):
        return lax.dynamic_slice_in_dim(w, start, size, axis)

    def own_rows(w):
        size = w.shape[0] // S
        return cut(w, s * size, size, 0)

    def gather_z(w):
        return lax.all_gather(w, "fsdp", axis=0, tiled=True)

    def reduce_z(w):
        return lax.psum_scatter(w, "fsdp", scatter_dimension=0, tiled=True)

    gains = jnp.pad(jnp.stack([gain_attn, gain_ffn], axis=1), ((0, 0), (0, 126)))
    kv = s // copies
    attn_part = jnp.concatenate(
        [
            cut(w_qkv, s * qw, qw, 1),
            cut(w_qkv, QW + kv * HD, HD, 1),
            cut(w_qkv, QW + KW + kv * HD, HD, 1),
            gains,
            own_rows(w_out).reshape(D // F, qw),
        ],
        axis=1,
    )
    attn_full = gather_z(attn_part)
    piece = FFs // F

    def own_columns(w):
        return cut(w.reshape(D // F, F, S, piece), s, 1, 2).reshape(D // F, FFs)

    gu_part = jnp.concatenate([own_columns(w_gate), own_columns(w_up)], axis=1)
    w_gu = gather_z(gu_part)
    w_dn = gather_z(own_rows(w_down))

    x_all = gather_sp(S, x_own, 0).reshape(L, D)
    frequency = 10000.0 ** (-2.0 * jnp.arange(HD // 2, dtype=f32) / HD)
    angles = frequency[:, None] * positions.astype(f32)
    cosine, sine = jnp.cos(angles), jnp.sin(angles)
    gain_q = gain_query.astype(f32)[:, None]
    gain_k = gain_key.astype(f32)[:, None]
    wqkv_s = attn_full[:, :hw]
    g_attn = attn_full[:, hw].astype(f32)[None]
    g_ffn = attn_full[:, hw + 1].astype(f32)[None]
    wout_s = attn_full[:, hw + 128 :].reshape(F, rows_o, D)
    normed_t, raw, rot, lse, mix_t, mix_all, wout_all = forward_attention(
        S, x_all, g_attn, wqkv_s, positions, cosine, sine, gain_q, gain_k, wout_s, heads, 1
    )
    wout_all = wout_all.reshape(S, qw, D)
    mid, ffn_in, ffn_t, ct_all = middle_rows(S, x_all, mix_all, wout_all, g_ffn, ct_own, 2)
    ct_all = ct_all.reshape(L, D)
    gate, up, hidden, part_down, wqkv_all = ffn_forward(S, ffn_in, ct_all, w_gu, wqkv_s, 3)
    grad_down = reduce_z(part_down)
    dgu, part_gu = ffn_backward(S, F, ct_all, w_dn, gate, up, ffn_t)
    grad_gu = reduce_z(part_gu.reshape(2 * D, FFs))
    gm, d_attn, grad_g_ffn, d_mix = middle_back(S, dgu, w_gu, wout_all, mid, g_ffn, ct_own, 4)
    d_proj, gain_sums, dattn_all = attention_back(
        S, ordered(d_mix, grad_down), rot, raw, lse, positions, cosine, sine, gain_q, gain_k, d_attn, heads, 5
    )
    part_out, part_qkv, grad_input, grad_g_attn = input_back(
        S, d_proj, mix_t, dattn_all.reshape(L, D), normed_t, wqkv_all, x_own, g_attn, gm, 6
    )

    W = 128
    n_q, n_o, n_g = S * rows_d * hw // W, rows_o * D // W, 16 * S
    small = jnp.concatenate([grad_g_attn, grad_g_ffn]).astype(bf16).reshape(2, S, F, rows_d)
    small = jnp.transpose(small, (2, 1, 0, 3)).reshape(F, S, 2 * rows_d)
    both = jnp.broadcast_to(gain_sums[:, :2].astype(bf16).T.reshape(1, 1, 2 * HD), (F, S, 2 * HD))
    small = jnp.concatenate([small, both], axis=2)
    small = jnp.pad(small, ((0, 0), (0, 0), (0, 16 * W - small.shape[2]))).reshape(F, n_g, W)
    part_qkv = jnp.transpose(part_qkv.reshape(S, F, rows_d, hw // W, W), (1, 0, 3, 2, 4)).reshape(F, n_q, W)
    part_out = jnp.transpose(part_out.reshape(F, rows_o, D // W, W), (0, 2, 1, 3)).reshape(F, n_o, W)
    packed = jnp.concatenate([part_qkv, part_out, small], axis=1).reshape(F * (n_q + n_o + n_g), W)
    mine = reduce_z(ordered(packed, grad_gu))
    out = output_rows(S, ordered(hidden, packed), w_dn, mid, 7)
    grad_gu = lax.all_to_all(grad_gu.reshape(S, 2, rows_d, FFs), "sp", split_axis=0, concat_axis=0)
    grad_out = jnp.swapaxes(mine[n_q : n_q + n_o].reshape(D // W, rows_o, W), 0, 1).reshape(rows_o, D).astype(f32)
    per_s = jnp.concatenate([mine[:n_q].reshape(S, n_q // S, W), mine[n_q + n_o :].reshape(S, 16, W)], axis=1)
    got = lax.all_to_all(per_s, "sp", split_axis=0, concat_axis=0)
    grad_qkv = jnp.swapaxes(got[:, :-16].reshape(S, hw // W, rows_d, W), 1, 2).reshape(S, rows_d, hw)
    tiny = jnp.sum(got[:, -16:].reshape(S, 16 * W)[:, : 2 * rows_d + 2 * HD].astype(f32), axis=0)
    grad_q = jnp.swapaxes(grad_qkv[:, :, :qw], 0, 1).reshape(rows_d, QW).astype(f32)
    grad_kv = jnp.sum(grad_qkv[:, :, qw:].reshape(KV_HEADS, copies, rows_d, 2, HD).astype(f32), axis=1)
    grad_kv = jnp.transpose(grad_kv, (1, 2, 0, 3)).reshape(rows_d, 2 * KW)
    grad_qkv = jnp.concatenate([grad_q, grad_kv], axis=1)
    grad_gu = jnp.transpose(grad_gu.reshape(S, 2, rows_d, F, piece), (1, 2, 3, 0, 4)).reshape(2, rows_d, FF).astype(f32)
    to_owner = [(i * F + j, j * S + i) for i in range(S) for j in range(F)]
    grad_down = lax.ppermute(grad_down, ("sp", "fsdp"), to_owner)
    return (
        out[None],
        grad_input[None],
        grad_qkv,
        grad_out,
        grad_gu[0],
        grad_gu[1],
        grad_down.astype(f32),
        tiny[:rows_d],
        tiny[rows_d : 2 * rows_d],
        tiny[2 * rows_d : 2 * rows_d + HD],
        tiny[2 * rows_d + HD :],
    )


def solution(mesh):
    row = P("fsdp", "sp", None)
    shard = P("fsdp", None)
    grad = P(("sp", "fsdp"), None)
    return jax.shard_map(
        local,
        mesh=mesh,
        in_specs=(row, shard, row, shard, shard, shard, shard, shard, P("fsdp"), P("fsdp"), P(), P()),
        out_specs=(row, row, grad, grad, grad, grad, grad, P(("sp", "fsdp")), P(("sp", "fsdp")), P(), P()),
        check_vma=False,
    )
```

time: 667 us -> 463 us (0.69)
  Pallas kernels: 0 us -> 370 us
  matrix products: 184 us -> 0 us
  waiting for transfers between devices: 170 us -> 3.72 us
  starting transfers between devices: 79 us -> 8.61 us
  other arithmetic: 67.1 us -> 9.37 us
  blocking collectives: 52.5 us -> 0 us
  local copies, waits for them, and re-layouts: 87.9 us -> 49.8 us
    pallas_call x0 -> x9, Pallas kernels: none -> 370 us  [the longest x1 59 us: output_rows(): pl.pallas_call(functools.partial(output_kernel, S), in_specs=[VMEM] * 3,...]
    dot_general x18 -> x0, matrix products: 184 us -> none  [the longest x3 31.1 us: times_transposed(): lax.dot_general(a, b, (((1,), (1,)), ((), ())), preferred_element_type=f32)]
    ppermute x34 -> x1, waiting for transfers between devices: 152 us -> 0.01 us  [local(): grad_down = lax.ppermute(grad_down, ('sp', 'fsdp'), to_owner)]
    ppermute x34 -> x1, starting transfers between devices: 63.3 us -> 0.87 us  [local(): grad_down = lax.ppermute(grad_down, ('sp', 'fsdp'), to_owner)]
    psum x1 -> x0, blocking collectives: 52.5 us -> none  [local(): tiny = lax.psum(tiny, ('sp', 'fsdp'))]
    dynamic_update_slice x17 -> x0, local copies, waits for them, and re-layouts: 27.5 us -> none  [gather_chunks(): stack = lax.dynamic_update_slice_in_dim(stack, part[None], s ^ mask, 0)]
    reduce_sum x9 -> x1, other arithmetic: 22.8 us -> 0.02 us  [local(): jnp.sum(got[:, -16:].reshape(S, 16 * W)[:, :2 * rows_d + 2 * HD].astype(f...]
    dynamic_update_slice x7 -> x0, other arithmetic: 14.7 us -> none  [the longest x6 9.39 us: gather_chunks(): return lax.dynamic_update_slice_in_dim(stack, across[None], s ^ 3, 0)]
  transfers between devices with their start and end apart: 46 -> 9, of which waited for: 25 -> 1; matrix products, arithmetic and copies ran while one was open for 31% -> 10% of each run, Pallas kernels for 0% -> 81%
where the time goes in v2:
time: 463 us; the launch traced here: 456 us
  Pallas kernels  370 us (80%)
  local copies, waits for them, and re-layouts  49.8 us (11%)
  between operations  14.8 us (3%)
  other arithmetic  9.37 us (2%)
  starting transfers between devices  8.61 us (2%)
    pallas_call x1, Pallas kernels, output_rows(): pl.pallas_call(functools.partial(output_kernel, S), in_specs=[VMEM] * 3,...  59 us
    pallas_call x1, Pallas kernels, middle_back(): pl.pallas_call(functools.partial(middle_back_kernel, S), in_specs=[VMEM]...  57.7 us
    pallas_call x1, Pallas kernels, forward_attention(): pl.pallas_call(functools.partial(forward_kernel, S, heads), grid=(steps,)...  42.9 us
    pallas_call x1, Pallas kernels, middle_rows(): pl.pallas_call(functools.partial(middle_kernel, S, T), grid=(S,), in_spec...  42.5 us
    pallas_call x1, Pallas kernels, attention_back(): pl.pallas_call(functools.partial(attn_back_kernel, S, heads), grid=(lengt...  40.4 us
    pallas_call x1, Pallas kernels, gather_sp(): pl.pallas_call(functools.partial(gather_kernel, S), in_specs=[ANY], out_s...  39.1 us
    pallas_call x1, Pallas kernels, ffn_forward(): pl.pallas_call(functools.partial(ffn_kernel, S), grid=(tiles,), in_specs=...  37.2 us
    pallas_call x1, Pallas kernels, ffn_backward(): pl.pallas_call(functools.partial(ffn_back_kernel, S, F), grid=(tiles,), i...  29.5 us
  transfers between devices with their start and end apart: 9, of which 1 were waited for; matrix products, arithmetic and copies ran while one was open for 10% of the time, Pallas kernels for 81%

profile of v2, /device:TPU:0, one launch (start us, length us, event | category | flops | bytes accessed | tf_op | source)
XLA Modules:
  0.0 456.3 jit_solution(8608324283241581064)
XLA Ops:
  12.7 4.4 reshape.165
  17.2 4.4 reshape.167
  21.6 8.6 %dynamic-slice_reduce_fusion = (bf16[256,8,128]{2,1,0:T(8,128)(2,1)S(1)}, bf16[256,8,128]{2,1,0:T(8,128)(2,1)S(1)}) fusion(bf16[256,8,4,128]{3,2,1,0:T(4,128)(2,1)} %reshape.167, s32[]{:T(128)S(6)} %select_n.26, bf16[256,8,4,128]{3,2,1,0:T(4,128)(2,1)} %reshape.165), kind=kLoop, calls=%fused_computation.4 | loop fusion | bytes 2097156 | tf_op jit(solution)/shard_map/dynamic_slice | solution.py:799
  34.2 39.1 %shard_map.203 = bf16[4,256,2048]{2,1,0:T(8,128)(2,1)} custom-call(bf16[256,2048]{1,0:T(8,128)(2,1)} %bitcast.90), custom_call_target="tpu_custom_call" | custom-call | bytes 162000000 | tf_op jit(solution)/shard_map/pallas_call | solution.py:174
  73.4 1.2 multiply_sine_fusion
  75.9 1.3 reshape.162.wout_ref
  77.2 2.9 slice.80.w_ref.wqkv_ref
  81.1 42.9 %shard_map.204 = (bf16[2048,1024]{1,0:T(8,128)(2,1)}, f32[384,1024]{1,0:T(8,128)}, bf16[384,1024]{1,0:T(8,128)(2,1)}, f32[8,1024]{1,0:T(8,128)}, bf16[256,1024]{...) custom-call(bf16[1024,2048]{1,0:T(8,128)(2,1)} %bitcast.77, f32[1,2048]{1,0:T(1,128)} %bitcast.112, ...), custom_call_target="tpu_custom_call" | custom-call | bytes 162000000 | tf_op jit(solution)/shard_map/pallas_call | solution.py:287
  124.0 42.5 %shard_map.205 = (f32[256,2048]{1,0:T(8,128)}, bf16[1024,2048]{1,0:T(8,128)(2,1)}, bf16[2048,1024]{1,0:T(8,128)(2,1)}, bf16[4,256,2048]{2,1,0:T(8,128)(2,1)}) custom-call(bf16[1024,2048]{1,0:T(8,128)(2,1)} %bitcast.78, bf16[4,1024,256]{2,1,0:T(8,128)(2,1)} %get-tuple-element.43.mix_ref, bf16[4,256,2048]{2,1,0:T(8,128)(2,1)} %bitcast.81, ...), custom_call_target="tpu_custom_call" | custom-call | bytes 162000000 | tf_op jit(solution)/shard_map/pallas_call | solution.py:366
  166.6 37.2 %shard_map.206 = (f32[1024,1024]{1,0:T(8,128)}, f32[1024,1024]{1,0:T(8,128)}, bf16[1024,1024]{1,0:T(8,128)(2,1)}, bf16[1024,2048]{1,0:T(8,128)(2,1)}, bf16[4,2048,384]{2,1,0:T(8,128)(2,1)}) custom-call(bf16[1024,2048]{1,0:T(8,128)(2,1)} %get-tuple-element.45.ffn_ref, bf16[1024,2048]{1,0:T(8,128)(2,1)} %bitcast.79, ...), custom_call_target="tpu_custom_call" | custom-call | bytes 72000000 | tf_op jit(solution)/shard_map/pallas_call | solution.py:416
  203.9 29.5 %shard_map.207 = (bf16[2,1024,1024]{2,1,0:T(8,128)(2,1)}, bf16[8,4,2,64,1024]{4,3,2,1,0:T(8,128)(2,1)}) custom-call(bf16[1024,2048]{1,0:T(8,128)(2,1)} %bitcast.80, bf16[1024,2048]{1,0:T(8,128)(2,1)} %all-gather.8.cloned.1.call-done.wd_ref, f32[1024,1024]{1,0:T(8,128)} %get-tuple-element.48.gate_ref, f32[1024,1024]{1,0:T(8,128)} %get-tuple-element.49.up_ref, ...), custom_call_target="tpu_custom_call" | custom-call | bytes 3600000 | tf_op jit(solution)/shard_map/pallas_call | solution.py:470
  233.6 57.7 %shard_map.208 = (f32[256,2048]{1,0:T(8,128)}, bf16[256,2048]{1,0:T(8,128)(2,1)}, f32[1,2048]{1,0:T(1,128)}, bf16[1024,256]{1,0:T(8,128)(2,1)}) custom-call(bf16[2,1024,1024]{2,1,0:T(8,128)(2,1)} %get-tuple-element.51.dgu_ref, bf16[2048,2048]{1,0:T(8,128)(2,1)} %all-gather.6.cloned.1.call-done.wg_ref.wu_ref.wgu_ref, bf16[4,256,2048]{2,1,0:T(8,128)(2,1)} %bitcast.82, ...), custom_call_target="tpu_custom_call" | custom-call | bytes 3600000 | tf_op jit(solution)/shard_map/pallas_call | solution.py:581
  292.1 40.4 %shard_map.209 = (bf16[1024,384]{1,0:T(8,128)(2,1)}, f32[64,128]{1,0:T(8,128)}, bf16[4,256,2048]{2,1,0:T(8,128)(2,1)}) custom-call(bf16[1024,256]{1,0:T(8,128)(2,1)} %get-tuple-element.55.dmix_ref, bf16[384,1024]{1,0:T(8,128)(2,1)} %get-tuple-element.56.rot_ref, f32[384,1024]{1,0:T(8,128)} %get-tuple-element.57.raw_ref, ...), custom_call_target="tpu_custom_call" | custom-call | bytes 3600000 | tf_op jit(solution)/shard_map/pallas_call | solution.py:675
  332.6 21.6 %shard_map.210 = (bf16[256,2048]{1,0:T(8,128)(2,1)}, bf16[2048,384]{1,0:T(8,128)(2,1)}, f32[256,2048]{1,0:T(8,128)}, f32[1,2048]{1,0:T(1,128)}) custom-call(bf16[1024,384]{1,0:T(8,128)(2,1)} %get-tuple-element.60.dproj_ref.dproj_hbm, bf16[1024,384]{1,0:T(8,128)(2,1)} %get-tuple-element.60.dproj_ref.dproj_hbm, bf16[256,1024]{1,0:T(8,128)(2,1)} %get-tuple-element.61.mix_t_ref, ...), custom_call_target="tpu_custom_call" | custom-call | bytes 3600000 | tf_op jit(solution)/shard_map/pallas_call | solution.py:729
  354.2 1.5 copy.92
  356.6 3.9 reshape.170
  361.0 1.8 pad_maximum_fusion
  362.8 3.7 all-to-all-start.1
  367.4 59.0 %shard_map.211 = bf16[256,2048]{1,0:T(8,128)(2,1)} custom-call(bf16[1024,1024]{1,0:T(8,128)(2,1)} %get-tuple-element.71.hid_ref, bf16[1024,2048]{1,0:T(8,128)(2,1)} %all-gather.8.cloned.1.call-done.wd_ref, f32[256,2048]{1,0:T(8,128)} %get-tuple-element.52.mid_ref), custom_call_target="tpu_custom_call" | custom-call | bytes 144000000 | tf_op jit(solution)/shard_map/pallas_call | solution.py:759
  428.6 1.4 squeeze.17
  430.7 1.4 squeeze.16
  434.5 3.4 all-to-all-start
  439.6 3.6 all-to-all-done
  446.1 3.2 copy.107
  (104 shorter events, 24.9 us)
Async XLA Ops:
  7.2 24.4 %copy-start = (bf16[512,2048]{1,0:T(8,128)(2,1)S(1)}, bf16[512,2048]{1,0:T(8,128)(2,1)}, u32[]{:S(2)}) copy-start(bf16[512,2048]{1,0:T(8,128)(2,1)} %param.19) | copy-start | bytes 6291460
  7.2 67.4 %all-gather.4.cloned.1.call-start = ((), (), s32[]{:S(2)}) async-start(), calls=%async_computation.5 | async-start | bytes 3538944 | tf_op jit(solution)/shard_map/all_gather | solution.py:806
  12.7 153.9 %all-gather.6.cloned.1.call-start = ((), (), s32[]{:S(2)}) async-start(), calls=%async_computation.6 | async-start | bytes 9437184 | tf_op jit(solution)/shard_map/all_gather | solution.py:806
  30.3 2.5 copy-start.4
  30.3 2.5 copy-start.8
  30.3 3.2 copy-start.9
  31.5 172.4 %all-gather.8.cloned.1.call-start = ((), (), s32[]{:S(2)}) async-start(), calls=%async_computation.7 | async-start | bytes 4718592 | tf_op jit(solution)/shard_map/all_gather | solution.py:806
  32.4 259.7 %reduce-scatter.4.cloned.1.call-start = ((), (), s32[]{:S(2)}) async-start(), calls=%async_computation.8 | async-start | bytes 4718592 | tf_op jit(solution)/shard_map/reduce_scatter | solution.py:809
  74.6 1.2 slice-start
  77.1 2.9 copy-start.2
  203.8 159.0 %reduce-scatter.6.cloned.1.call-start = ((), (), s32[]{:S(2)}) async-start(), calls=%async_computation.9 | async-start | bytes 9437184 | tf_op jit(solution)/shard_map/reduce_scatter | solution.py:809
  233.4 198.7 %reduce-scatter.8.cloned.1.call-start = ((), (), s32[]{:S(2)}) async-start(), calls=%async_computation.10 | async-start | bytes 3096576 | tf_op jit(solution)/shard_map/reduce_scatter | solution.py:809
  354.2 1.8 copy-start.5
  354.2 2.0 copy-start.6
  362.8 3.7 copy-start.7
  362.8 64.7 %all-to-all-start.1 = ((bf16[4,2,64,1024]{3,2,1,0:T(8,128)(2,1)}), bf16[4,2,64,1024]{3,2,1,0:T(8,128)(2,1)S(1)}, u32[]{:S(2)}, u32[]{:S(2)}) async-start(bf16[4,2,64,1024]{3,2,1,0:T(8,128)(2,1)} %bitcast.27), calls=%async_computation.4 | async-start | bytes 2097152 | tf_op jit(solution)/shard_map/all_to_all | solution.py:873
  366.5 59.9 %collective-permute-start = (bf16[128,2048]{1,0:T(8,128)(2,1)S(1)}, bf16[128,2048]{1,0:T(8,128)(2,1)S(1)}, u32[]{:S(2)}, u32[]{:S(2)}) collective-permute-start(bf16[128,2048]{1,0:T(8,128)(2,1)S(1)} %copy-done.7), channel_id=1, source_target_pairs={{0,0},{1,4},{2,8},{3,12},{4,16},{5,20},{6,24},{7,28},{8,1},{9,5},{... | collective-permute-start | bytes 1572872 | tf_op jit(solution)/shard_map/ppermute | solution.py:885
  432.1 13.0 %copy-start.3 = (bf16[256,2048]{1,0:T(8,128)(2,1)S(1)}, bf16[256,2048]{1,0:T(8,128)(2,1)}, u32[]{:S(2)}) copy-start(bf16[256,2048]{1,0:T(8,128)(2,1)} %shard_map.211) | copy-start | bytes 3145732
  434.5 8.6 %all-to-all-start = ((bf16[4,208,128]{2,1,0:T(8,128)(2,1)}), bf16[4,208,128]{2,1,0:T(8,128)(2,1)S(1)}, u32[]{:S(2)}, u32[]{:S(2)}) async-start(bf16[4,208,128]{2,1,0:T(8,128)(2,1)} %pad_maximum_fusion.2), calls=%async_computation.3 | async-start | bytes 425984 | tf_op jit(solution)/shard_map/all_to_all | solution.py:876
  445.1 4.1 copy-start.1
Sparse Core Ops, SparseCore 0:
  12.8 40.9 all-gather.3
  56.0 80.9 all-gather.5
  139.1 45.6 all-gather.7
  203.9 50.0 reduce-scatter.3
  256.1 87.7 reduce-scatter.5
  363.0 52.3 reduce-scatter.7
